TPU v7x, 32 devices: a whole 2x2x4 slice. The times are simulated.
32 devices in a mesh: parts: 2 (over x), loop: 16 (over z, y, core).
Axes of the slice: x: 2, y: 2, z: 4, core: 2. Of those that a mesh axis runs over, the one named last changes fastest.
Arguments:
- classes: int32 [256], P(('parts', 'loop')), parts along dimension 0, may hold values from 0 to 2
- forward_field: bfloat16 [256, 512, 128], P(('parts', 'loop')), parts along dimension 0, may hold values from -6 to 6
- adjoint_source: bfloat16 [256, 512, 128], P(('parts', 'loop')), parts along dimension 0, may hold values from -6 to 6
- leaf_solve: bfloat16 [6, 2, 512, 512], P('parts'), parts along dimension 0, may hold values from -0.1875 to 0.1875
- leaf_lift: bfloat16 [6, 2, 512, 128], P('parts'), parts along dimension 0, may hold values from -0.375 to 0.375
- leaf_skeleton: bfloat16 [6, 2, 128, 512], P('parts'), parts along dimension 0, may hold values from -0.1875 to 0.1875
- block_merge: bfloat16 [16, 2, 128, 128], P('parts'), parts along dimension 0, may hold values from -0.125 to 0.125
- block_split: bfloat16 [16, 2, 128, 128], P('parts'), parts along dimension 0, may hold values from -0.375 to 0.375
- level_up: bfloat16 [8, 2, 128, 256], P('parts'), parts along dimension 0, may hold values from -0.25 to 0.25
- level_down: bfloat16 [8, 2, 256, 256], P('parts'), parts along dimension 0, may hold values from -0.25 to 0.25
- level_parent: bfloat16 [8, 2, 256, 128], P('parts'), parts along dimension 0, may hold values from -0.375 to 0.375
- root_solve: bfloat16 [4, 128, 128], P('parts'), parts along dimension 0, may hold values from -0.375 to 0.375
- rim_left: bfloat16 [6, 2, 128, 128], P('parts'), parts along dimension 0, may hold values from -0.375 to 0.375
- rim_right: bfloat16 [6, 2, 128, 128], P('parts'), parts along dimension 0, may hold values from -0.375 to 0.375
- shape_derivative: float32 [6, 2, 512], P('parts'), parts along dimension 0, may hold values from -6 to 6
- illum_angle: float32 [256], P('parts'), parts along dimension 0, may hold values from -3.140625 to 3.140625
- illum_weight: float32 [256], P('parts'), parts along dimension 0, may hold values from 0.3 to 3
- illum_ids: int32 [64], replicated, may hold values from 0 to 127
Outputs:
- adjoint: bfloat16 [256, 512, 128], P(('parts', 'loop')), parts along dimension 0
- gradient: float32 [256], P(('parts', 'loop')), parts along dimension 0
There are 2 independent parts, one for each index of `parts`. A program takes and returns all parts, laid end to end along the dimension named above; an argument that names none is the same for every part. Nothing has to cross between parts.
Inputs may be any that keep to these rules, and one draw needn't show every extreme that they name: `illum_ids`: which of the 128 tabulated illuminations each adjoint belongs to.
All inputs are finite; a program needn't handle non-finite values.
Results may differ from a plain program's by a relative error of at most 0.007.
Values may be sent and summed in bfloat16 or wider, within the bound.
No kernel may reach another device: no remote copies, remote signals or barrier semaphores. Data moves between devices by JAX's collectives and lax.ppermute only.
A program may use at most 128 MiB of HBM per device.

v0:
```python
import math

import jax
import jax.numpy as jnp
from jax import lax
from jax.sharding import PartitionSpec as P

PRECISE = lax.Precision.HIGHEST


def partner_2(value, axis, stride):
    mask = 2**stride
    pairs = [(source, source ^ mask) for source in range(lax.axis_size(axis))]
    return lax.ppermute(value, axis, pairs)


def extended(x, sides, width):
    for axis, dim in sides:
        count, length = (lax.axis_size(axis), x.shape[dim])
        up = [(i, (i + 1) % count) for i in range(count)]
        down = [(j, i) for i, j in up]
        last = lax.slice_in_dim(x, length - width, length, axis=dim)
        first = lax.slice_in_dim(x, 0, width, axis=dim)
        before = lax.ppermute(last, axis, up)
        after = lax.ppermute(first, axis, down)
        x = jnp.concatenate([before, x, after], axis=dim)
    return x


def rotate_half(values):
    middle = values.shape[-1] // 2
    return jnp.concatenate([-values[..., middle:], values[..., :middle]], axis=-1)


def complex_exact(matrix, block):
    wide = matrix.astype(jnp.float32)
    direct = jnp.dot(wide[0], block, precision=PRECISE, preferred_element_type=jnp.float32)
    twisted = jnp.dot(wide[1], block, precision=PRECISE, preferred_element_type=jnp.float32)
    return direct + rotate_half(twisted)


def batch_product(matrices, blocks):
    direct = jnp.einsum("brc,bck->brk", matrices[:, 0], blocks, preferred_element_type=jnp.float32)
    twisted = jnp.einsum("brc,bck->brk", matrices[:, 1], blocks, preferred_element_type=jnp.float32)
    return direct + rotate_half(twisted)


def phase_turn(values, cosine, sine_values):
    middle = values.shape[-1] // 2
    real_part = values[..., :middle]
    imag_part = values[..., middle:]
    return jnp.concatenate(
        [
            real_part * cosine - imag_part * sine_values,
            real_part * sine_values + imag_part * cosine,
        ],
        axis=-1,
    )


def shards(
    classes,
    forward_field,
    adjoint_source,
    leaf_solve,
    leaf_lift,
    leaf_skeleton,
    block_merge,
    block_split,
    level_up,
    level_down,
    level_parent,
    root_solve,
    rim_left,
    rim_right,
    shape_derivative,
    illum_angle,
    illum_weight,
    illum_ids,
):
    position = lax.axis_index("loop")
    device_count = lax.axis_size("loop")
    rank = root_solve.shape[-1]
    width = forward_field.shape[-1]
    illum = width // 2
    nodes = forward_field.shape[1]
    rim = rim_left.shape[-1]
    levels = level_up.shape[0]
    skeleton_cells = batch_product(leaf_skeleton[classes], adjoint_source)
    merge_wide = block_merge.astype(jnp.float32)
    block_source = jnp.einsum(
        "prc,pck->rk", merge_wide[:, 0], skeleton_cells, precision=PRECISE
    ) + rotate_half(jnp.einsum("prc,pck->rk", merge_wide[:, 1], skeleton_cells, precision=PRECISE))
    local_part = batch_product(leaf_solve[classes], adjoint_source)
    lower_list = []
    higher_list = []
    current = block_source
    for level in range(levels):
        partner = partner_2(current, "loop", level)
        upper_bit = position >> level & 1
        lower = jnp.where(upper_bit == 1, partner, current)
        higher = jnp.where(upper_bit == 1, current, partner)
        lower_list.append(lower)
        higher_list.append(higher)
        current = complex_exact(level_up[level], jnp.concatenate([lower, higher], axis=0))
    field = complex_exact(root_solve, current)
    for level in reversed(range(levels)):
        children = complex_exact(
            level_down[level], jnp.concatenate([lower_list[level], higher_list[level]], axis=0)
        ) + complex_exact(level_parent[level], field)
        upper_bit = position >> level & 1
        field = jnp.where(upper_bit == 1, children[rank:], children[:rank])
    split_wide = block_split.astype(jnp.float32)
    cell_field = jnp.einsum(
        "prc,ck->prk", split_wide[:, 0], field, precision=PRECISE
    ) + rotate_half(jnp.einsum("prc,ck->prk", split_wide[:, 1], field, precision=PRECISE))
    cell_field = cell_field.astype(jnp.bfloat16)
    adjoint = (local_part + batch_product(leaf_lift[classes], cell_field)).astype(jnp.bfloat16)
    table_size = illum_angle.shape[0]
    one_hot = (illum_ids[:, None] == jnp.arange(table_size, dtype=jnp.int32)[None, :]).astype(
        jnp.float32
    )
    angles = jnp.dot(one_hot, illum_angle, precision=PRECISE)
    weights = jnp.dot(one_hot, illum_weight, precision=PRECISE)
    cosine = jnp.cos(angles)
    sine_values = jnp.sin(angles)
    padded = extended(forward_field, (("loop", 0),), 1)
    left_in = padded[:-2, nodes - rim :]
    right_in = padded[2:, :rim]
    left_term = batch_product(rim_left[classes], left_in)
    right_term = batch_product(rim_right[classes], right_in)
    at_start = position == 0
    at_end = position == device_count - 1
    first_left = jnp.where(at_start, phase_turn(left_term[0], cosine, -sine_values), left_term[0])
    left_term = jnp.concatenate([first_left[None], left_term[1:]], axis=0)
    final_right = jnp.where(at_end, phase_turn(right_term[-1], cosine, sine_values), right_term[-1])
    right_term = jnp.concatenate([right_term[:-1], final_right[None]], axis=0)
    derivative = shape_derivative[classes]
    field_wide = forward_field.astype(jnp.float32)
    real_part = field_wide[..., :illum]
    imag_part = field_wide[..., illum:]
    deriv_real = derivative[:, 0, :, None]
    deriv_imag = derivative[:, 1, :, None]
    perturbed = jnp.concatenate(
        [
            deriv_real * real_part - deriv_imag * imag_part,
            deriv_real * imag_part + deriv_imag * real_part,
        ],
        axis=-1,
    )
    perturbed = jnp.concatenate(
        [
            perturbed[:, :rim] + left_term,
            perturbed[:, rim : nodes - rim],
            perturbed[:, nodes - rim :] + right_term,
        ],
        axis=1,
    )
    adjoint_wide = adjoint.astype(jnp.float32)
    pointwise = (
        adjoint_wide[..., :illum] * perturbed[..., :illum]
        - adjoint_wide[..., illum:] * perturbed[..., illum:]
    )
    gradient = jnp.dot(jnp.sum(pointwise, axis=1), weights, precision=PRECISE) / math.sqrt(
        nodes * illum
    )
    return (adjoint, gradient)


def solution(mesh):
    return jax.shard_map(
        shards,
        mesh=mesh,
        in_specs=(
            P(("parts", "loop")),
            P(("parts", "loop"), None, None),
            P(("parts", "loop"), None, None),
            P("parts", None, None, None),
            P("parts", None, None, None),
            P("parts", None, None, None),
            P("parts", None, None, None),
            P("parts", None, None, None),
            P("parts", None, None, None),
            P("parts", None, None, None),
            P("parts", None, None, None),
            P("parts", None, None),
            P("parts", None, None, None),
            P("parts", None, None, None),
            P("parts", None, None),
            P("parts"),
            P("parts"),
            P(),
        ),
        out_specs=(P(("parts", "loop"), None, None), P(("parts", "loop"))),
        check_vma=False,
    )
```

profile of v0, /device:TPU:0, one launch (start us, length us, event | category | flops | bytes accessed | tf_op | source)
XLA Modules:
  0.0 86.9 jit_solution(4187958447678005004)
XLA Ops:
  1.5 3.3 %gather_fusion.2 = bf16[8,2,128,512]{3,2,1,0:T(8,128)(2,1)} fusion(bf16[3,2,128,512]{3,2,1,0:T(8,128)(2,1)} %param.23, s32[1024]{0:T(1024)S(1)} %pad_clamp_fusion), kind=kCustom, calls=%fused_computation.2 | custom fusion | bytes 4194336 | tf_op jit(solution)/shard_map/gather | solution.py:89
  4.8 2.1 %fusion.29 = f32[8,128,128]{2,1,0:T(8,128)S(1)} fusion(bf16[8,512,128]{2,1,0:T(8,128)(2,1)} %param.20, bf16[8,2,128,512]{3,2,1,0:T(8,128)(2,1)} %gather_fusion.2), kind=kOutput, calls=%fused_computation.83 | convolution fusion | flops 134217728 | bytes 2621440 | tf_op jit(solution)/shard_map/brc,bck->brk/dot_general | solution.py:44
  10.2 2.3 %copy.96 = bf16[8,512,128]{1,2,0:T(8,128)(2,1)} copy(bf16[8,512,128]{2,1,0:T(8,128)(2,1)} %param.19) | data formatting | bytes 2097152 | tf_op args[1]
  12.4 1.7 %fusion.116 = (bf16[1,512,128]{1,2,0:T(8,128)(2,1)}, bf16[1,512,128]{1,2,0:T(8,128)(2,1)}) fusion(bf16[8,512,128]{1,2,0:T(8,128)(2,1)} %copy.96), kind=kLoop, calls=%fused_computation.228 | loop fusion | bytes 524288 | tf_op jit(solution)/shard_map/slice | solution.py:22
  14.2 5.6 %collective-permute-start.5 = (bf16[1,512,128]{1,2,0:T(8,128)(2,1)}, bf16[1,512,128]{1,2,0:T(8,128)(2,1)}, u32[]{:S(2)}, u32[]{:S(2)}) collective-permute-start(bf16[1,512,128]{1,2,0:T(8,128)(2,1)} %get-tuple-element.17), channel_id=1, source_target_pairs={{1,0},{2,1},{3,2},{4,3},{5,4},{6,5},{7,6},{8,7},{9,8},{10,9},{11,1... | collective-permute-start | bytes 393224 | tf_op jit(solution)/shard_map/ppermute | solution.py:25
  19.8 4.6 %gather_fusion = bf16[8,2,512,512]{3,2,1,0:T(8,128)(2,1)} fusion(bf16[3,2,512,512]{3,2,1,0:T(8,128)(2,1)S(1)} %copy-done, s32[1024]{0:T(1024)S(1)} %pad_clamp_fusion), kind=kCustom, calls=%fused_computation | custom fusion | bytes 16777248 | tf_op jit(solution)/shard_map/gather | solution.py:94
  24.4 5.4 %fusion.1 = f32[8,512,128]{1,2,0:T(8,128)} fusion(bf16[8,512,128]{2,1,0:T(8,128)(2,1)} %param.20, bf16[8,2,512,512]{3,2,1,0:T(8,128)(2,1)} %gather_fusion), kind=kOutput, calls=%fused_computation.9 | convolution fusion | flops 536870912 | bytes 7340032 | tf_op jit(solution)/shard_map/brc,bck->brk/dot_general | solution.py:43
  29.8 3.8 %fusion = f32[8,512,128]{1,2,0:T(8,128)S(1)} fusion(bf16[8,512,128]{2,1,0:T(8,128)(2,1)S(1)} %copy-done.10, bf16[8,2,512,512]{3,2,1,0:T(8,128)(2,1)} %gather_fusion), kind=kOutput, calls=%fused_computation.7 | convolution fusion | flops 536870912 | bytes 7340032 | tf_op jit(solution)/shard_map/brc,bck->brk/dot_general | solution.py:44
  33.6 1.6 %convert_element_type.11 = f32[8,512,128]{1,2,0:T(8,128)} convert(bf16[8,512,128]{1,2,0:T(8,128)(2,1)S(1)} %copy-done.1) | non-fusion elementwise | flops 524288 | bytes 3145728 | tf_op jit(solution)/shard_map/convert_element_type | solution.py:139
  35.3 1.5 %slice_negate_fusion.1 = (f32[8,512,64]{1,2,0:T(8,128)}, f32[8,512,64]{1,2,0:T(8,128)}) fusion(f32[8,512,128]{1,2,0:T(8,128)S(1)} %fusion), kind=kLoop, calls=%fused_computation.86 | loop fusion | flops 262144 | bytes 4194304 | tf_op jit(solution)/shard_map/neg | solution.py:32
  37.9 1.9 %multiply_subtract_fusion = (f32[8,512,64]{1,2,0:T(8,128)S(1)}, f32[8,512,64]{1,2,0:T(8,128)S(1)}) fusion(f32[8,512,128]{1,2,0:T(8,128)} %convert_element_type.11, f32[8,512]{1,0:T(8,128)S(1)} %get-tuple-element.75, f32[8,512]{1,0:T(8,128)S(1)} %get-tuple-element.76), kind=kLoop, calls=%fused_computation.88 | loop fusion | flops 1572864 | bytes 4227072 | tf_op jit(solution)/shard_map/sub | solution.py:146
  40.8 1.1 %fusion.25 = f32[8,256,128]{1,2,0:T(8,128)} fusion(f32[8,512,64]{1,2,0:T(8,128)S(1)} %get-tuple-element.6, f32[8,512,64]{1,2,0:T(8,128)S(1)} %get-tuple-element.7), kind=kLoop, calls=%fused_computation.74 | loop fusion | flops 262144 | bytes 3145728 | tf_op jit(solution)/shard_map/concatenate | solution.py:144
  41.9 3.3 %gather_fusion.1 = bf16[8,2,512,128]{3,2,1,0:T(8,128)(2,1)} fusion(bf16[3,2,512,128]{3,2,1,0:T(8,128)(2,1)} %param.22, s32[1024]{0:T(1024)S(1)} %pad_clamp_fusion), kind=kCustom, calls=%fused_computation.1 | custom fusion | bytes 4194336 | tf_op jit(solution)/shard_map/gather | solution.py:118
  45.2 1.4 %gather_fusion.4 = bf16[8,2,128,128]{3,2,1,0:T(8,128)(2,1)} fusion(bf16[3,2,128,128]{3,2,1,0:T(8,128)(2,1)S(1)} %copy-done.17, s32[1024]{0:T(1024)S(1)} %pad_clamp_fusion), kind=kCustom, calls=%fused_computation.4 | custom fusion | bytes 1048608 | tf_op jit(solution)/shard_map/gather | solution.py:130
  46.6 1.4 %gather_fusion.5 = bf16[8,2,128,128]{3,2,1,0:T(8,128)(2,1)} fusion(bf16[3,2,128,128]{3,2,1,0:T(8,128)(2,1)S(1)} %copy-done.18, s32[1024]{0:T(1024)S(1)} %pad_clamp_fusion), kind=kCustom, calls=%fused_computation.5 | custom fusion | bytes 1048608 | tf_op jit(solution)/shard_map/gather | solution.py:131
  50.3 1.1 %fusion.22 = f32[128,128]{1,0:T(8,128)S(1)} fusion(f32[128,64]{1,0:T(8,128)S(1)} %get-tuple-element.63, f32[128,64]{1,0:T(8,128)S(1)} %get-tuple-element.62, bf16[4,2,128,256]{3,2,1,0:T(8,128)(2,1)} %param.26, f32[128,128]{1,0:T(8,128)S(1)} %get-tuple-element.49, f32[128,128]{1,0:T(8,128)S(1)} %get-tuple-element.48), kind=kOutput, calls=%fused_computation.66 | convolution fusion | flops 50397184 | bytes 327680 | tf_op jit(solution)/shard_map/dot_general | solution.py:37
  51.5 1.2 %convolution_bitcast_fusion.16 = f32[256,128]{1,0:T(8,128)S(1)} fusion(bf16[4,2,256,256]{3,2,1,0:T(8,128)(2,1)} %param.27, f32[128,128]{1,0:T(8,128)S(1)} %get-tuple-element.49, f32[128,128]{1,0:T(8,128)S(1)} %get-tuple-element.48), kind=kOutput, calls=%fused_computation.42 | convolution fusion | flops 100696064 | bytes 393216 | tf_op jit(solution)/shard_map/dot_general | solution.py:38
  52.8 3.0 %collective-permute-done.1 = f32[128,128]{1,0:T(8,128)S(1)} collective-permute-done((f32[128,128]{1,0:T(8,128)S(1)}, f32[128,128]{1,0:T(8,128)S(1)}, u32[]{:S(2)}, u32[]{:S(2)}) %collective-permute-start.1) | collective-permute-done | bytes 65568 | tf_op jit(solution)/shard_map/ppermute | solution.py:14
  60.6 1.1 %copy-done.11 = f32[8,256,128]{1,2,0:T(8,128)S(1)} copy-done((f32[8,256,128]{1,2,0:T(8,128)S(1)}, f32[8,256,128]{1,2,0:T(8,128)}, u32[]{:S(2)}) %copy-start.11) | copy-done | bytes 1048600
  61.7 1.6 %pad_maximum_fusion = f32[8,512,128]{1,2,0:T(8,128)} fusion(f32[8,128,128]{1,2,0:T(8,128)S(1)} %get-tuple-element.9, f32[8,256,128]{1,2,0:T(8,128)S(1)} %copy-done.11, f32[8,128,128]{1,2,0:T(8,128)S(1)} %get-tuple-element.8), kind=kLoop, calls=%fused_computation.16 | loop fusion | flops 1048576 | bytes 4194304 | tf_op jit(solution)/shard_map/concatenate | solution.py:151
  65.9 4.8 %collective-permute-done.3 = f32[128,128]{1,0:T(8,128)S(1)} collective-permute-done((f32[128,128]{1,0:T(8,128)S(1)}, f32[128,128]{1,0:T(8,128)S(1)}, u32[]{:S(2)}, u32[]{:S(2)}) %collective-permute-start.3) | collective-permute-done | bytes 65568 | tf_op jit(solution)/shard_map/ppermute | solution.py:14
  79.3 2.2 %fusion.119 = (f32[8,512,128]{1,2,0:T(8,128)}, bf16[8,512,128]{1,2,0:T(8,128)(2,1)}) fusion(f32[8,512,64]{1,2,0:T(8,128)S(1)} %get-tuple-element.11, f32[8,512,64]{1,2,0:T(8,128)S(1)} %get-tuple-element.10, bf16[8,128,128]{1,2,0:T(8,128)(2,1)S(1)} %fusion.5, bf16[8,2,512,128]{3,2,1,0:T(8,128)(2,1)S(1)} %copy-done.8, f32[8,512,128]{1,2,0:T(8,128)S(1)} %copy-done.14, ...), kind=kOutput, calls=%fused_computation.231 | convolution fusion | flops 137887744 | bytes 10747904 | tf_op jit(solution)/shard_map/brc,bck->brk/dot_general | solution.py:43
  81.5 2.3 %copy.105 = bf16[8,512,128]{2,1,0:T(8,128)(2,1)} copy(bf16[8,512,128]{1,2,0:T(8,128)(2,1)} %get-tuple-element.74) | data formatting | bytes 2097152
  83.8 2.4 %fusion.27 = f32[8,64]{1,0:T(8,128)S(1)} fusion(f32[8,512,128]{1,2,0:T(8,128)} %pad_maximum_fusion, f32[8,512,128]{1,2,0:T(8,128)} %get-tuple-element.73), kind=kLoop, calls=%fused_computation.77 | loop fusion | flops 1048064 | bytes 4196352 | tf_op jit(solution)/shard_map/reduce_sum | solution.py:164
  (140 shorter events, 24.8 us)
Async XLA Ops:
  0.6 19.2 %copy-start = (bf16[3,2,512,512]{3,2,1,0:T(8,128)(2,1)S(1)}, bf16[3,2,512,512]{3,2,1,0:T(8,128)(2,1)}, u32[]{:S(2)}) copy-start(bf16[3,2,512,512]{3,2,1,0:T(8,128)(2,1)} %param.21) | copy-start | bytes 9437188
  4.7 2.3 %copy-start.7 = (bf16[8,2,128,512]{3,2,1,0:T(8,128)(2,1)S(1)}, bf16[8,2,128,512]{3,2,1,0:T(8,128)(2,1)}, u32[]{:S(2)}) copy-start(bf16[8,2,128,512]{3,2,1,0:T(8,128)(2,1)} %gather_fusion.2) | copy-start | bytes 6291460
  4.7 2.5 %copy-start.9 = (bf16[8,512,128]{2,1,0:T(8,128)(2,1)S(1)}, bf16[8,512,128]{2,1,0:T(8,128)(2,1)}, u32[]{:S(2)}) copy-start(bf16[8,512,128]{2,1,0:T(8,128)(2,1)} %param.20) | copy-start | bytes 3145732
  9.7 38.4 %collective-permute-start = (f32[128,128]{1,0:T(8,128)}, f32[128,128]{1,0:T(8,128)}, u32[]{:S(2)}, u32[]{:S(2)}) collective-permute-start(f32[128,128]{1,0:T(8,128)} %fusion.23), channel_id=1, source_target_pairs={{0,1},{1,0},{2,3},{3,2},{4,5},{5,4},{6,7},{7,6},{8,9},{9,8},{10,11... | collective-permute-start | bytes 196616 | tf_op jit(solution)/shard_map/ppermute | solution.py:14
  14.1 42.2 %collective-permute-start.4 = (bf16[1,512,128]{1,2,0:T(8,128)(2,1)}, bf16[1,512,128]{1,2,0:T(8,128)(2,1)}, u32[]{:S(2)}, u32[]{:S(2)}) collective-permute-start(bf16[1,512,128]{1,2,0:T(8,128)(2,1)} %get-tuple-element.16), channel_id=1, source_target_pairs={{0,1},{1,2},{2,3},{3,4},{4,5},{5,6},{6,7},{7,8},{8,9},{9,10},{10,1... | collective-permute-start | bytes 393224 | tf_op jit(solution)/shard_map/ppermute | solution.py:24
  14.2 42.1 %collective-permute-start.5 = (bf16[1,512,128]{1,2,0:T(8,128)(2,1)}, bf16[1,512,128]{1,2,0:T(8,128)(2,1)}, u32[]{:S(2)}, u32[]{:S(2)}) collective-permute-start(bf16[1,512,128]{1,2,0:T(8,128)(2,1)} %get-tuple-element.17), channel_id=1, source_target_pairs={{1,0},{2,1},{3,2},{4,3},{5,4},{6,5},{7,6},{8,7},{9,8},{10,9},{11,1... | collective-permute-start | bytes 393224 | tf_op jit(solution)/shard_map/ppermute | solution.py:25
  24.4 5.4 %copy-start.10 = (bf16[8,512,128]{2,1,0:T(8,128)(2,1)S(1)}, bf16[8,512,128]{2,1,0:T(8,128)(2,1)}, u32[]{:S(2)}) copy-start(bf16[8,512,128]{2,1,0:T(8,128)(2,1)} %param.20) | copy-start | bytes 3145732
  29.8 3.8 %copy-start.1 = (bf16[8,512,128]{1,2,0:T(8,128)(2,1)S(1)}, bf16[8,512,128]{1,2,0:T(8,128)(2,1)}, u32[]{:S(2)}) copy-start(bf16[8,512,128]{1,2,0:T(8,128)(2,1)} %copy.96) | copy-start | bytes 3145732
  35.3 2.2 %copy-start.26 = (f32[128]{0:T(128)S(1)}, f32[128]{0:T(128)}, u32[]{:S(2)}) copy-start(f32[128]{0:T(128)} %param.33) | copy-start | bytes 1540
  35.3 2.2 %copy-start.27 = (s32[64]{0:T(128)S(1)}, s32[64]{0:T(128)}, u32[]{:S(2)}) copy-start(s32[64]{0:T(128)} %param.35) | copy-start | bytes 772
  35.3 2.5 %copy-start.28 = (f32[128]{0:T(128)S(1)}, f32[128]{0:T(128)}, u32[]{:S(2)}) copy-start(f32[128]{0:T(128)} %param.34) | copy-start | bytes 1540
  39.8 2.1 %copy-start.5 = (f32[8,512,64]{1,2,0:T(8,128)}, f32[8,512,64]{1,2,0:T(8,128)S(1)}, u32[]{:S(2)}) copy-start(f32[8,512,64]{1,2,0:T(8,128)S(1)} %get-tuple-element.7) | copy-start | bytes 3145732
  41.9 3.3 %copy-start.17 = (bf16[3,2,128,128]{3,2,1,0:T(8,128)(2,1)S(1)}, bf16[3,2,128,128]{3,2,1,0:T(8,128)(2,1)}, u32[]{:S(2)}) copy-start(bf16[3,2,128,128]{3,2,1,0:T(8,128)(2,1)} %param.30) | copy-start | bytes 589828
  41.9 4.7 %copy-start.18 = (bf16[3,2,128,128]{3,2,1,0:T(8,128)(2,1)S(1)}, bf16[3,2,128,128]{3,2,1,0:T(8,128)(2,1)}, u32[]{:S(2)}) copy-start(bf16[3,2,128,128]{3,2,1,0:T(8,128)(2,1)} %param.31) | copy-start | bytes 589828
  48.1 7.7 %copy-start.19 = (bf16[4,2,256,256]{3,2,1,0:T(8,128)(2,1)S(1)}, bf16[4,2,256,256]{3,2,1,0:T(8,128)(2,1)}, u32[]{:S(2)}) copy-start(bf16[4,2,256,256]{3,2,1,0:T(8,128)(2,1)} %param.27) | copy-start | bytes 3145732
  48.1 8.0 %copy-start.23 = (bf16[4,2,128,256]{3,2,1,0:T(8,128)(2,1)S(1)}, bf16[4,2,128,256]{3,2,1,0:T(8,128)(2,1)}, u32[]{:S(2)}) copy-start(bf16[4,2,128,256]{3,2,1,0:T(8,128)(2,1)} %param.26) | copy-start | bytes 1572868
  48.1 8.2 %copy-start.2 = (bf16[8,512,128]{1,2,0:T(8,128)(2,1)S(1)}, bf16[8,512,128]{1,2,0:T(8,128)(2,1)}, u32[]{:S(2)}) copy-start(bf16[8,512,128]{1,2,0:T(8,128)(2,1)} %copy.96) | copy-start | bytes 3145732
  50.3 6.9 %copy-start.16 = (bf16[8,2,128,128]{3,2,1,0:T(8,128)(2,1)S(1)}, bf16[8,2,128,128]{3,2,1,0:T(8,128)(2,1)}, u32[]{:S(2)}) copy-start(bf16[8,2,128,128]{3,2,1,0:T(8,128)(2,1)} %gather_fusion.4) | copy-start | bytes 1572868
  51.4 4.3 %collective-permute-start.1 = (f32[128,128]{1,0:T(8,128)S(1)}, f32[128,128]{1,0:T(8,128)S(1)}, u32[]{:S(2)}, u32[]{:S(2)}) collective-permute-start(f32[128,128]{1,0:T(8,128)S(1)} %fusion.22), channel_id=1, source_target_pairs={{0,2},{1,3},{2,0},{3,1},{4,6},{5,7},{6,4},{7,5},{8,10},{9,11},{10,... | collective-permute-start | bytes 196616 | tf_op jit(solution)/shard_map/ppermute | solution.py:14
  59.6 4.3 %collective-permute-start.2 = (f32[128,128]{1,0:T(8,128)S(1)}, f32[128,128]{1,0:T(8,128)S(1)}, u32[]{:S(2)}, u32[]{:S(2)}) collective-permute-start(f32[128,128]{1,0:T(8,128)S(1)} %fusion.21), channel_id=1, source_target_pairs={{0,4},{1,5},{2,6},{3,7},{4,0},{5,1},{6,2},{7,3},{8,12},{9,13},{10,... | collective-permute-start | bytes 196616 | tf_op jit(solution)/shard_map/ppermute | solution.py:14
  63.3 8.3 %copy-start.25 = (bf16[2,128,128]{2,1,0:T(8,128)(2,1)S(1)}, bf16[2,128,128]{2,1,0:T(8,128)(2,1)}, u32[]{:S(2)}) copy-start(bf16[2,128,128]{2,1,0:T(8,128)(2,1)} %param.29) | copy-start | bytes 196612
  63.3 8.8 %copy-start.22 = (bf16[4,2,256,128]{3,2,1,0:T(8,128)(2,1)S(1)}, bf16[4,2,256,128]{3,2,1,0:T(8,128)(2,1)}, u32[]{:S(2)}) copy-start(bf16[4,2,256,128]{3,2,1,0:T(8,128)(2,1)} %param.28) | copy-start | bytes 1572868
  64.8 5.9 %collective-permute-start.3 = (f32[128,128]{1,0:T(8,128)S(1)}, f32[128,128]{1,0:T(8,128)S(1)}, u32[]{:S(2)}, u32[]{:S(2)}) collective-permute-start(f32[128,128]{1,0:T(8,128)S(1)} %fusion.20), channel_id=1, source_target_pairs={{0,8},{1,9},{2,10},{3,11},{4,12},{5,13},{6,14},{7,15},{8,0},{9,1},... | collective-permute-start | bytes 196616 | tf_op jit(solution)/shard_map/ppermute | solution.py:14
  77.1 2.2 %copy-start.14 = (f32[8,512,128]{1,2,0:T(8,128)S(1)}, f32[8,512,128]{1,2,0:T(8,128)}, u32[]{:S(2)}) copy-start(f32[8,512,128]{1,2,0:T(8,128)} %fusion.1) | copy-start | bytes 6291460
  (11 other events, 14.7 us)
where the time goes:
time: 87.5 us; the launch traced here: 86.9 us
  matrix products  27.7 us (32%)
  local copies, waits for them, and re-layouts  27.1 us (31%)
  other arithmetic  14.9 us (17%)
  waiting for transfers between devices  8.4 us (10%)
  starting transfers between devices  7.32 us (8%)
  between operations  1.37 us (2%)
    unnamed x61, local copies, waits for them, and re-layouts  10.6 us
    dot_general x5, matrix products, batch_product(): jnp.einsum('brc,bck->brk', matrices[:, 0], blocks, preferred_element_type...  8.57 us
    ppermute x4, waiting for transfers between devices, partner_2(): return lax.ppermute(value, axis, pairs)  8.39 us
    dot_general x5, matrix products, batch_product(): jnp.einsum('brc,bck->brk', matrices[:, 1], blocks, preferred_element_type...  6.93 us
    ppermute x1, starting transfers between devices, extended(): after = lax.ppermute(first, axis, down)  5.64 us
    dot_general x13, matrix products, complex_exact(): jnp.dot(wide[1], block, precision=PRECISE, preferred_element_type=jnp.flo...  4.86 us
    gather x1, local copies, waits for them, and re-layouts, shards(): local_part = batch_product(leaf_solve[classes], adjoint_source)  4.63 us
    dot_general x13, matrix products, complex_exact(): jnp.dot(wide[0], block, precision=PRECISE, preferred_element_type=jnp.flo...  4.05 us
  transfers between devices with their start and end apart: 6, of which 3 were waited for; matrix products, arithmetic and copies ran while one was open for 44% of the time, Pallas kernels for 0%

commit v1 on v0

v1 whole, which is shorter than its diff:
```python
import functools
import math

import jax
import jax.numpy as jnp
from jax import lax
from jax.experimental import pallas as pl
from jax.experimental.pallas import tpu as pltpu
from jax.sharding import PartitionSpec as P

F32 = jnp.float32
BF16 = jnp.bfloat16
MIB = 1 << 20
VM = pl.BlockSpec(memory_space=pltpu.VMEM)
SM = pl.BlockSpec(memory_space=pltpu.SMEM)
ANY = pl.BlockSpec(memory_space=pl.ANY)


def params(mib):
    return pltpu.CompilerParams(vmem_limit_bytes=mib * MIB)


def cost(flops, nbytes):
    return pl.CostEstimate(flops=flops, bytes_accessed=nbytes, transcendentals=0)


def half_sign(width):
    lane = lax.broadcasted_iota(jnp.int32, (1, width), 1)
    return jnp.where(lane < width // 2, -1.0, 1.0).astype(F32)


def turn(values):
    width = values.shape[-1]
    return pltpu.roll(values, width // 2, 1) * half_sign(width)


def dot(a, b):
    return jnp.dot(a, b, preferred_element_type=F32)


def split(x):
    high = x.astype(BF16)
    return high, (x - high.astype(F32)).astype(BF16)


def embed(re, im):
    return jnp.concatenate(
        [jnp.concatenate([re, -im], axis=1), jnp.concatenate([im, re], axis=1)], axis=0
    )


def times(re, im, stacked):
    left = embed(re, im)
    if stacked.dtype == BF16:
        return dot(left, stacked)
    high, low = split(stacked)
    return dot(left, high) + dot(left, low)


def side_by_side(stacked):
    rows = stacked.shape[0] // 2
    return jnp.concatenate([stacked[:rows], stacked[rows:]], axis=1)


def groups_of(levels):
    return [tuple(range(low, min(low + 2, levels))) for low in range(0, levels, 2)]


def pair_of(ref, level):
    return ref[level, 0], ref[level, 1]


def up_map(group, up_ref, left_of):
    rank = up_ref.shape[2]
    bottom = jnp.concatenate([up_ref[group[0], 0], up_ref[group[0], 1]], axis=0)
    re, im = left_of
    return jnp.concatenate(
        [
            times(re[:, j * rank : (j + 1) * rank], im[:, j * rank : (j + 1) * rank], bottom)
            for j in range(2)
        ],
        axis=1,
    )


def rows_of(ref, level, bit):
    rank = ref.shape[2] // 2
    start = pl.multiple_of(bit * rank, rank)
    return ref[level, 0, pl.ds(start, rank), :], ref[level, 1, pl.ds(start, rank), :]


def group_maps(group, position, up_ref, down_ref, parent_ref):
    low = group[0]
    low_bit = (position >> low) & 1
    parent_re, parent_im = rows_of(parent_ref, low, low_bit)
    down_re, down_im = rows_of(down_ref, low, low_bit)
    local = jnp.concatenate([down_re, down_im], axis=0).astype(F32)
    if len(group) == 1:
        up = jnp.concatenate([up_ref[low, 0], up_ref[low, 1]], axis=0)
        return up.astype(F32), local, jnp.concatenate([parent_re, parent_im], axis=0).astype(F32)
    high = group[1]
    high_bit = (position >> high) & 1
    w = up_map(group, up_ref, pair_of(up_ref, high))
    inner = up_map(group, up_ref, rows_of(down_ref, high, high_bit))
    outer = times(parent_re, parent_im, inner)
    placed = jnp.concatenate(
        [
            local * jnp.where(high_bit == 0, 1.0, 0.0).astype(F32),
            local * jnp.where(high_bit == 1, 1.0, 0.0).astype(F32),
        ],
        axis=1,
    )
    top_re, top_im = rows_of(parent_ref, high, high_bit)
    q = times(parent_re, parent_im, jnp.concatenate([top_re, top_im], axis=0))
    return w, outer + placed, q


def up_kernel(scal, source, skeleton, merge, forward, out, even, odd, src_v, skel_v, merge_v, sems):
    cells = src_v.shape[0]
    classes = skel_v.shape[0]
    rim = even.shape[0]
    nodes = forward.shape[1]
    parity = scal[cells] & 1
    copies = []

    def start(src, dst, i):
        c = pltpu.make_async_copy(src, dst, sems.at[i])
        c.start()
        copies.append(c)

    for k in range(classes):
        start(skeleton.at[k], skel_v.at[k], k)
    for p in range(cells):
        start(source.at[p], src_v.at[p], classes + p)
    start(merge, merge_v, classes + cells)
    last = (cells - 1, nodes - rim)
    even_cell = jnp.where(parity == 0, last[0], 0)
    even_row = pl.multiple_of(jnp.where(parity == 0, last[1], 0), rim)
    odd_cell = jnp.where(parity == 1, last[0], 0)
    odd_row = pl.multiple_of(jnp.where(parity == 1, last[1], 0), rim)
    start(forward.at[even_cell, pl.ds(even_row, rim), :], even, classes + cells + 1)
    start(forward.at[odd_cell, pl.ds(odd_row, rim), :], odd, classes + cells + 2)
    for k in range(classes):
        copies[k].wait()
    pieces = []
    for p in range(cells):
        copies[classes + p].wait()
        k = scal[p]
        v = src_v[p]
        weights = jnp.concatenate([skel_v[k, 0], skel_v[k, 1]], axis=0)
        rank = skel_v.shape[2]
        both = dot(weights, v)
        pieces.append((both[:rank] + turn(both[rank:])).astype(BF16))
    copies[classes + cells].wait()
    total = None
    rank = skel_v.shape[2]
    for p in range(0, cells, 2):
        mine = range(p, min(p + 2, cells))
        left = jnp.concatenate(
            [
                jnp.concatenate([merge_v[i, 0] for i in mine], axis=1),
                jnp.concatenate([merge_v[i, 1] for i in mine], axis=1),
            ],
            axis=0,
        )
        term = dot(left, jnp.concatenate([pieces[i] for i in mine], axis=0))
        total = term if total is None else total + term
    out[...] = (total[:rank] + turn(total[rank:])).astype(BF16)
    copies[classes + cells + 1].wait()
    copies[classes + cells + 2].wait()


def local_kernel(scal, source, solve, up_ref, down_ref, parent_ref, _, local, maps, *, groups):
    cells = source.shape[0]
    position = scal[cells]
    rank = up_ref.shape[2]
    for g, group in enumerate(groups[:-1]):
        w, f, _q = group_maps(group, position, up_ref, down_ref, parent_ref)
        columns = 2 * w.shape[1]
        maps[g, :rank, :columns] = side_by_side(w).astype(BF16)
        maps[g, rank:, :columns] = side_by_side(f).astype(BF16)

    @pl.loop(0, cells)
    def _loop(p):
        k = scal[p]
        v = source[p]
        turned = turn(v.astype(F32)).astype(BF16)
        left = jnp.concatenate([solve[k, 0], solve[k, 1]], axis=1)
        local[p] = dot(left, jnp.concatenate([v, turned], axis=0))


def gather_nodes(group, position, own, arrived, nodes_v):
    count = 1 << len(group)
    rank = own.shape[0]
    index = (position >> group[0]) & (count - 1)
    for mask in range(count):
        value = own[...] if mask == 0 else arrived[mask - 1][...]
        where = index ^ mask
        nodes_v[where] = value
        nodes_v[count + where] = turn(value.astype(F32)).astype(BF16)
    return nodes_v[: 2 * count].reshape(2 * count * rank, own.shape[1])


def combine_kernel(scal, maps, own, *refs, group, index, cells):
    count = 1 << len(group)
    arrived = refs[: count - 1]
    node, part, nodes_v = refs[count - 1 :]
    rank = own.shape[0]
    stack = gather_nodes(group, scal[cells], own, arrived, nodes_v)
    both = dot(maps[index, :, : stack.shape[0]], stack)
    node[...] = both[:rank].astype(BF16)
    part[...] = both[rank:]


def perturb_kernel(
    scal,
    forward,
    even,
    odd,
    rim_left,
    rim_right,
    shape_ref,
    angle_ref,
    weight_ref,
    ids_ref,
    up_ref,
    down_ref,
    parent_ref,
    root_ref,
    _,
    weighted,
    final_map,
    columns,
    *,
    groups,
    device_count,
):
    cells, nodes, width = forward.shape
    rim = even.shape[0]
    classes = shape_ref.shape[0]
    position = scal[cells]
    parity = position & 1

    w, f, q = group_maps(groups[-1], position, up_ref, down_ref, parent_ref)
    top = times(root_ref[0], root_ref[1], w)
    rank = root_ref.shape[1]
    high, low = split(q)
    top_high, top_low = split(top)
    left = embed(high[:rank], high[rank:])
    extra = embed(low[:rank], low[rank:])
    total = f + dot(left, top_high) + dot(left, top_low) + dot(extra, top_high)
    for group in reversed(groups[:-1]):
        for level in reversed(group):
            re, im = rows_of(parent_ref, level, (position >> level) & 1)
            total = times(re, im, total)
    final_map[...] = side_by_side(total).astype(BF16)

    ids = jnp.concatenate([ids_ref[...], ids_ref[...]], axis=1)
    table = angle_ref.shape[1]
    chosen = lax.broadcasted_iota(jnp.int32, (table, width), 0) == ids

    def column_of(row):
        return jnp.transpose(jnp.broadcast_to(row, (8, table)))[:, :1]

    angles = jnp.sum(jnp.where(chosen, column_of(angle_ref[...]), 0.0), axis=0, keepdims=True)
    weights = jnp.sum(jnp.where(chosen, column_of(weight_ref[...]), 0.0), axis=0, keepdims=True)
    weights = weights * half_sign(width) * (-1.0 / math.sqrt(nodes * (width // 2)))
    cosine = jnp.cos(angles)
    sine = jnp.sin(angles)

    for k in range(classes):
        turned = jnp.transpose(jnp.concatenate([shape_ref[k]] * 4, axis=0))
        columns[k, 0] = jnp.broadcast_to(turned[:, 0:1], (nodes, width)) * weights
        columns[k, 1] = jnp.broadcast_to(turned[:, 1:2], (nodes, width)) * weights

    def rim_term(ref, k, block):
        both = dot(jnp.concatenate([ref[k, 0], ref[k, 1]], axis=0), block)
        return both[:rim] + turn(both[rim:])

    def phase_turn(values, active, sign):
        c = jnp.where(active, cosine, 1.0)
        s = jnp.where(active, sine * sign, 0.0)
        return values * c + turn(values) * s

    before = jnp.where(parity == 1, even[...], odd[...])
    after = jnp.where(parity == 0, even[...], odd[...])
    for p in range(cells):
        k = scal[p]
        field = forward[p].astype(F32)
        value = columns[k, 0] * field + columns[k, 1] * turn(field)
        left_in = before if p == 0 else forward[p - 1, nodes - rim :, :]
        right_in = after if p == cells - 1 else forward[p + 1, :rim, :]
        left_term = rim_term(rim_left, k, left_in)
        right_term = rim_term(rim_right, k, right_in)
        if p == 0:
            left_term = phase_turn(left_term, position == 0, -1.0)
        if p == cells - 1:
            right_term = phase_turn(right_term, position == device_count - 1, 1.0)
        weighted[p, :rim, :] = value[:rim] + left_term * weights
        weighted[p, rim : nodes - rim, :] = value[rim : nodes - rim]
        weighted[p, nodes - rim :, :] = value[nodes - rim :] + right_term * weights


def down_kernel(scal, final_map, own, *refs, group, cells):
    count = 1 << len(group)
    arrived = refs[: count - 1]
    part, split_ref, lift, local, weighted, adjoint, gradient, nodes_v, out_v, sems = refs[count - 1 :]
    rank = own.shape[0]
    width = own.shape[1]
    stack = gather_nodes(group, scal[cells], own, arrived, nodes_v)
    field = dot(final_map[...], stack) + part[...]
    both = jnp.concatenate([field.astype(BF16), turn(field).astype(BF16)], axis=0)
    copies = []
    sums = []
    for p in range(cells):
        k = scal[p]
        cell = dot(jnp.concatenate([split_ref[p, 0], split_ref[p, 1]], axis=1), both)
        rhs = jnp.concatenate([cell.astype(BF16), turn(cell).astype(BF16)], axis=0)
        value = local[p] + dot(jnp.concatenate([lift[k, 0], lift[k, 1]], axis=1), rhs)
        rounded = value.astype(BF16)
        out_v[p] = rounded
        c = pltpu.make_async_copy(out_v.at[p], adjoint.at[p], sems.at[p])
        c.start()
        copies.append(c)
        sums.append(jnp.sum(rounded.astype(F32) * weighted[p], axis=0, keepdims=True))
    table = jnp.sum(jnp.concatenate(sums, axis=0), axis=1, keepdims=True)
    row = lax.broadcasted_iota(jnp.int32, (cells, cells), 0)
    lane = lax.broadcasted_iota(jnp.int32, (cells, cells), 1)
    gradient[...] = jnp.sum(jnp.where(row == lane, table, 0.0), axis=0, keepdims=True)
    for c in copies:
        c.wait()


def shards(
    classes,
    forward_field,
    adjoint_source,
    leaf_solve,
    leaf_lift,
    leaf_skeleton,
    block_merge,
    block_split,
    level_up,
    level_down,
    level_parent,
    root_solve,
    rim_left,
    rim_right,
    shape_derivative,
    illum_angle,
    illum_weight,
    illum_ids,
):
    position = lax.axis_index("loop")
    device_count = lax.axis_size("loop")
    cells, nodes, width = adjoint_source.shape
    class_count = leaf_solve.shape[0]
    rank = root_solve.shape[-1]
    rim = rim_left.shape[-1]
    levels = level_up.shape[0]
    groups = groups_of(levels)
    scal = jnp.concatenate([classes, position.astype(jnp.int32)[None]])
    sds = jax.ShapeDtypeStruct
    node = sds((rank, width), BF16)

    source, even, odd = pl.pallas_call(
        up_kernel,
        out_shape=(node, sds((rim, width), BF16), sds((rim, width), BF16)),
        in_specs=[SM, ANY, ANY, ANY, ANY],
        out_specs=(VM, VM, VM),
        scratch_shapes=[
            pltpu.VMEM((cells, nodes, width), BF16),
            pltpu.VMEM((class_count, 2, rank, nodes), BF16),
            pltpu.VMEM(block_merge.shape, BF16),
            pltpu.SemaphoreType.DMA((class_count + cells + 3,)),
        ],
        compiler_params=params(12),
        cost_estimate=cost(4 * cells * rank * nodes * width, 3 * MIB),
        name="up",
    )(scal, adjoint_source, leaf_skeleton, block_merge, forward_field)

    def exchange(value, mask):
        pairs = [(i, i ^ mask) for i in range(device_count)]
        return lax.ppermute(value, "loop", pairs)

    def odd_exchange(value):
        pairs = [
            (i, (i + 1) % device_count if i % 2 else (i - 1) % device_count)
            for i in range(device_count)
        ]
        return lax.ppermute(value, "loop", pairs)

    def gather(value, group):
        base = 1 << group[0]
        return [exchange(value, base * m) for m in range(1, 1 << len(group))]

    even_in = exchange(even, 1)
    arrived = gather(source, groups[0])
    odd_in = odd_exchange(odd)

    most = 2 * (rank << 2)
    local, maps = pl.pallas_call(
        functools.partial(local_kernel, groups=groups),
        out_shape=(
            sds((cells, nodes, width), F32),
            sds((max(len(groups) - 1, 1), 2 * rank, most), BF16),
        ),
        in_specs=[SM] + [VM] * 6,
        out_specs=(VM, VM),
        compiler_params=params(8),
        cost_estimate=cost(8 * cells * nodes * nodes * width, 6 * MIB),
        name="local",
    )(scal, adjoint_source, leaf_solve, level_up, level_down, level_parent, source)

    own = source
    fields = []
    for g, group in enumerate(groups[:-1]):
        count = 1 << len(group)
        own, part = pl.pallas_call(
            functools.partial(combine_kernel, group=group, index=g, cells=cells),
            out_shape=(node, sds((rank, width), F32)),
            in_specs=[SM] + [VM] * (1 + count),
            out_specs=(VM, VM),
            scratch_shapes=[pltpu.VMEM((2 * count, rank, width), BF16)],
            compiler_params=params(4),
            cost_estimate=cost(16 * rank * rank * width, MIB),
            name="combine",
        )(scal, maps, own, *arrived)
        fields.append((group, part))
        arrived = gather(own, groups[g + 1])

    weighted, final_map = pl.pallas_call(
        functools.partial(perturb_kernel, groups=groups, device_count=device_count),
        out_shape=(
            sds((cells, nodes, width), F32),
            sds((rank, 2 * (rank << len(groups[-1]))), BF16),
        ),
        in_specs=[SM] + [VM] * 14,
        out_specs=(VM, VM),
        scratch_shapes=[pltpu.VMEM((class_count, 2, nodes, width), F32)],
        compiler_params=params(10),
        cost_estimate=cost(8 * cells * rim * rim * width, 4 * MIB),
        name="perturb",
    )(
        scal,
        forward_field,
        even_in,
        odd_in,
        rim_left,
        rim_right,
        shape_derivative,
        illum_angle[None],
        illum_weight[None],
        illum_ids[None],
        level_up,
        level_down,
        level_parent,
        root_solve,
        own,
    )

    part = fold_parts(fields, level_parent, position, rank, width)
    group = groups[-1]
    count = 1 << len(group)
    adjoint, gradient = pl.pallas_call(
        functools.partial(down_kernel, group=group, cells=cells),
        out_shape=(sds((cells, nodes, width), BF16), sds((1, cells), F32)),
        in_specs=[SM] + [VM] * (count + 1 + 5),
        out_specs=(ANY, VM),
        scratch_shapes=[
            pltpu.VMEM((2 * count, rank, width), BF16),
            pltpu.VMEM((cells, nodes, width), BF16),
            pltpu.SemaphoreType.DMA((cells,)),
        ],
        compiler_params=params(8),
        cost_estimate=cost(8 * cells * nodes * rank * width, 8 * MIB),
        name="down",
    )(scal, final_map, own, *arrived, part, block_split, leaf_lift, local, weighted)
    return adjoint, gradient[0]


def fold_parts(fields, level_parent, position, rank, width):
    if not fields:
        return jnp.zeros((rank, width), F32)
    total = fields[-1][1]
    for group, part in reversed(fields[:-1]):
        for level in reversed(group):
            start = ((position >> level) & 1) * rank
            rows = lax.dynamic_slice_in_dim(level_parent[level], start, rank, 1).astype(F32)
            direct = jnp.dot(rows[0], total, precision=lax.Precision.HIGHEST)
            twisted = jnp.dot(rows[1], total, precision=lax.Precision.HIGHEST)
            half = width // 2
            total = direct + jnp.concatenate([-twisted[:, half:], twisted[:, :half]], axis=1)
        total = total + part
    return total


def solution(mesh):
    return jax.shard_map(
        shards,
        mesh=mesh,
        in_specs=(
            P(("parts", "loop")),
            P(("parts", "loop"), None, None),
            P(("parts", "loop"), None, None),
            P("parts", None, None, None),
            P("parts", None, None, None),
            P("parts", None, None, None),
            P("parts", None, None, None),
            P("parts", None, None, None),
            P("parts", None, None, None),
            P("parts", None, None, None),
            P("parts", None, None, None),
            P("parts", None, None),
            P("parts", None, None, None),
            P("parts", None, None, None),
            P("parts", None, None),
            P("parts"),
            P("parts"),
            P(),
        ),
        out_specs=(P(("parts", "loop"), None, None), P(("parts", "loop"))),
        check_vma=False,
    )
```

time: 87.5 us -> 38.7 us (0.44)
  matrix products: 27.7 us -> 0 us
  local copies, waits for them, and re-layouts: 27.1 us -> 6.57 us
  Pallas kernels: 0 us -> 17.6 us
  other arithmetic: 14.9 us -> 0.73 us
  waiting for transfers between devices: 8.4 us -> 0.02 us
  starting transfers between devices: 7.32 us -> 12.6 us
    dot_general x43 -> x0, matrix products: 27.7 us -> none  [the longest x5 8.57 us: batch_product(): jnp.einsum('brc,bck->brk', matrices[:, 0], blocks, preferred_element_type...]
    pallas_call x0 -> x5, Pallas kernels: none -> 17.6 us  [the longest x1 5.09 us: shards(): pl.pallas_call(functools.partial(local_kernel, groups=groups), out_shape=...]
    gather x6 -> x0, local copies, waits for them, and re-layouts: 14.7 us -> none  [the longest x1 4.63 us: shards(): local_part = batch_product(leaf_solve[classes], adjoint_source)]
    ppermute x6 -> x8, waiting for transfers between devices: 8.4 us -> 0.02 us  [the longest x7 0.02 us: exchange(): return lax.ppermute(value, 'loop', pairs)]
    ppermute x6 -> x8, starting transfers between devices: 7.32 us -> 12.6 us  [the longest x7 8.1 us: exchange(): return lax.ppermute(value, 'loop', pairs)]
    unnamed x61 -> x38, local copies, waits for them, and re-layouts: 10.6 us -> 6.57 us
    neg x21 -> x0, other arithmetic: 3.21 us -> none  [the longest x20 3.21 us: rotate_half(): -values[..., middle:]]
    concatenate x4 -> x1, other arithmetic: 3.7 us -> 0.73 us  [shards(): scal = jnp.concatenate([classes, position.astype(jnp.int32)[None]])]
  transfers between devices with their start and end apart: 6 -> 8, of which waited for: 3 -> 0; matrix products, arithmetic and copies ran while one was open for 44% -> 0% of each run, Pallas kernels for 0% -> 23%
where the time goes in v1:
time: 38.7 us; the launch traced here: 38.4 us
  Pallas kernels  17.6 us (45%)
  starting transfers between devices  12.6 us (33%)
  local copies, waits for them, and re-layouts  6.57 us (17%)
  between operations  0.86 us (2%)
  other arithmetic  0.73 us (2%)
    ppermute x7, starting transfers between devices, exchange(): return lax.ppermute(value, 'loop', pairs)  8.1 us
    unnamed x38, local copies, waits for them, and re-layouts  6.57 us
    pallas_call x1, Pallas kernels, shards(): pl.pallas_call(functools.partial(local_kernel, groups=groups), out_shape=...  5.09 us
    pallas_call x1, Pallas kernels, shards(): pl.pallas_call(up_kernel, out_shape=(node, sds((rim, width), BF16), sds((...  4.86 us
    ppermute x1, starting transfers between devices, odd_exchange(): return lax.ppermute(value, 'loop', pairs)  4.49 us
    pallas_call x1, Pallas kernels, shards(): pl.pallas_call(functools.partial(down_kernel, group=group, cells=cells),...  3.83 us
    pallas_call x1, Pallas kernels, shards(): pl.pallas_call(functools.partial(perturb_kernel, groups=groups, device_co...  2.91 us
    pallas_call x1, Pallas kernels, shards(): pl.pallas_call(functools.partial(combine_kernel, group=group, index=g, ce...  0.93 us
  transfers between devices with their start and end apart: 8, of which 0 were waited for; matrix products, arithmetic and copies ran while one was open for 0% of the time, Pallas kernels for 23%

profile of v1, /device:TPU:0, one launch (start us, length us, event | category | flops | bytes accessed | tf_op | source)
XLA Modules:
  0.0 38.4 jit_solution(5169040940715120243)
XLA Ops:
  0.6 0.7 %pad_add_fusion.scal = s32[9]{0:T(128)S(1)} fusion(s32[1]{0:T(128)} %bitcast, s32[8]{0:T(128)} %param.18), kind=kLoop, calls=%fused_computation | loop fusion | flops 9 | bytes 72 | tf_op jit(solution)/shard_map/concatenate | solution.py:362
  1.4 1.2 %copy-done = bf16[8,512,128]{2,1,0:T(8,128)(2,1)S(1)} copy-done((bf16[8,512,128]{2,1,0:T(8,128)(2,1)S(1)}, bf16[8,512,128]{2,1,0:T(8,128)(2,1)}, u32[]{:S(2)}) %copy-start) | copy-done | bytes 1048600
  2.6 1.2 %copy-done.2 = bf16[8,512,128]{2,1,0:T(8,128)(2,1)S(1)} copy-done((bf16[8,512,128]{2,1,0:T(8,128)(2,1)S(1)}, bf16[8,512,128]{2,1,0:T(8,128)(2,1)}, u32[]{:S(2)}) %copy-start.2) | copy-done | bytes 1048600
  3.8 1.1 %copy-done.6 = bf16[3,2,128,512]{3,2,1,0:T(8,128)(2,1)S(1)} copy-done((bf16[3,2,128,512]{3,2,1,0:T(8,128)(2,1)S(1)}, bf16[3,2,128,512]{3,2,1,0:T(8,128)(2,1)}, u32[]{:S(2)}) %copy-start.6) | copy-done | bytes 786456
  4.9 1.0 %copy-done.8 = bf16[8,2,128,128]{3,2,1,0:T(8,128)(2,1)S(1)} copy-done((bf16[8,2,128,128]{3,2,1,0:T(8,128)(2,1)S(1)}, bf16[8,2,128,128]{3,2,1,0:T(8,128)(2,1)}, u32[]{:S(2)}) %copy-start.8) | copy-done | bytes 524312
  6.0 4.9 %up.1 = (bf16[128,128]{1,0:T(8,128)(2,1)S(1)}, bf16[128,128]{1,0:T(8,128)(2,1)S(1)}, bf16[128,128]{1,0:T(8,128)(2,1)S(1)}) custom-call(s32[9]{0:T(128)S(1)} %pad_add_fusion.scal, bf16[8,512,128]{2,1,0:T(8,128)(2,1)S(1)} %copy-done.2, bf16[3,2,128,512]{3,2,1,0:T(8,128)(2,1)S(1)} %copy-done.6, bf16[8,2,128,128]{3,2,1,0:T(8,128)(2,1)S(1)} %copy-done.8, ...), custom_call_target="tpu_custom_call" | custom-call | flops 268435456 | bytes 3145728 | tf_op jit(solution)/shard_map/up/pallas_call | solution.py:366
  10.9 2.5 %collective-permute-start.4 = (bf16[128,128]{1,0:T(8,128)(2,1)S(1)}, bf16[128,128]{1,0:T(8,128)(2,1)S(1)}, u32[]{:S(2)}, u32[]{:S(2)}) collective-permute-start(bf16[128,128]{1,0:T(8,128)(2,1)S(1)} %get-tuple-element.15._.own), channel_id=1, source_target_pairs={{0,3},{1,2},{2,1},{3,0},{4,7},{5,6},{6,5},{7,4},{8,11},{9,10},{10,... | collective-permute-start | bytes 98312 | tf_op jit(solution)/shard_map/ppermute | solution.py:384
  13.4 0.6 %collective-permute-start.3 = (bf16[128,128]{1,0:T(8,128)(2,1)S(1)}, bf16[128,128]{1,0:T(8,128)(2,1)S(1)}, u32[]{:S(2)}, u32[]{:S(2)}) collective-permute-start(bf16[128,128]{1,0:T(8,128)(2,1)S(1)} %get-tuple-element.15._.own), channel_id=1, source_target_pairs={{0,2},{1,3},{2,0},{3,1},{4,6},{5,7},{6,4},{7,5},{8,10},{9,11},{10,... | collective-permute-start | bytes 98312 | tf_op jit(solution)/shard_map/ppermute | solution.py:384
  14.0 0.0 collective-permute-start.2
  14.0 0.5 %collective-permute-start = (bf16[128,128]{1,0:T(8,128)(2,1)S(1)}, bf16[128,128]{1,0:T(8,128)(2,1)S(1)}, u32[]{:S(2)}, u32[]{:S(2)}) collective-permute-start(bf16[128,128]{1,0:T(8,128)(2,1)S(1)} %get-tuple-element.13), channel_id=1, source_target_pairs={{0,1},{1,0},{2,3},{3,2},{4,5},{5,4},{6,7},{7,6},{8,9},{9,8},{10,11... | collective-permute-start | bytes 98312 | tf_op jit(solution)/shard_map/ppermute | solution.py:384
  14.5 0.0 copy-start.14
  14.5 0.0 copy-start.15
  14.5 0.0 copy-start.16
  14.6 0.0 copy-start.17
  14.6 4.5 %collective-permute-start.1 = (bf16[128,128]{1,0:T(8,128)(2,1)S(1)}, bf16[128,128]{1,0:T(8,128)(2,1)S(1)}, u32[]{:S(2)}, u32[]{:S(2)}) collective-permute-start(bf16[128,128]{1,0:T(8,128)(2,1)S(1)} %get-tuple-element.14), channel_id=1, source_target_pairs={{0,15},{1,2},{2,1},{3,4},{4,3},{5,6},{6,5},{7,8},{8,7},{9,10},{10,... | collective-permute-start | bytes 98312 | tf_op jit(solution)/shard_map/ppermute | solution.py:391
  19.1 0.0 copy-start.18
  19.1 1.9 %copy-done.18 = bf16[3,2,512,512]{3,2,1,0:T(8,128)(2,1)S(1)} copy-done((bf16[3,2,512,512]{3,2,1,0:T(8,128)(2,1)S(1)}, bf16[3,2,512,512]{3,2,1,0:T(8,128)(2,1)}, u32[]{:S(2)}) %copy-start.18) | copy-done | bytes 3145752
  21.0 5.1 %local.1 = (f32[8,512,128]{2,1,0:T(8,128)S(1)}, bf16[1,256,1024]{2,1,0:T(8,128)(2,1)S(1)}) custom-call(s32[9]{0:T(128)S(1)} %pad_add_fusion.scal, bf16[8,512,128]{2,1,0:T(8,128)(2,1)S(1)} %copy-done.3, bf16[3,2,512,512]{3,2,1,0:T(8,128)(2,1)S(1)} %copy-done.18, bf16[4,2,128,256]{3,2,1,0:T(8,128)(2,1)S(1)} %copy-done.9, ...), custom_call_target="tpu_custom_call" | custom-call | flops 2147483648 | bytes 6291456 | tf_op jit(solution)/shard_map/local/pallas_call | solution.py:402
  26.1 0.0 copy-start.7
  26.1 0.9 %combine.1 = (bf16[128,128]{1,0:T(8,128)(2,1)S(1)}, f32[128,128]{1,0:T(8,128)S(1)}) custom-call(s32[9]{0:T(128)S(1)} %pad_add_fusion.scal, bf16[1,256,1024]{2,1,0:T(8,128)(2,1)S(1)} %get-tuple-element.16.maps, bf16[128,128]{1,0:T(8,128)(2,1)S(1)} %get-tuple-element.15._.own, bf16[128,128]{1,0:T(8,128)(2,1)S(1)} %collective-permute-done.2.refs_0_, ...), custom_call_target="tpu_custom_call" | custom-call | flops 33554432 | bytes 1048576 | tf_op jit(solution)/shard_map/combine/pallas_call | solution.py:419
  27.1 0.5 %collective-permute-start.7 = (bf16[128,128]{1,0:T(8,128)(2,1)S(1)}, bf16[128,128]{1,0:T(8,128)(2,1)S(1)}, u32[]{:S(2)}, u32[]{:S(2)}) collective-permute-start(bf16[128,128]{1,0:T(8,128)(2,1)S(1)} %get-tuple-element.17._.own), channel_id=1, source_target_pairs={{0,12},{1,13},{2,14},{3,15},{4,8},{5,9},{6,10},{7,11},{8,4},{9,5},... | collective-permute-start | bytes 98312 | tf_op jit(solution)/shard_map/ppermute | solution.py:384
  27.6 3.9 %collective-permute-start.5 = (bf16[128,128]{1,0:T(8,128)(2,1)S(1)}, bf16[128,128]{1,0:T(8,128)(2,1)S(1)}, u32[]{:S(2)}, u32[]{:S(2)}) collective-permute-start(bf16[128,128]{1,0:T(8,128)(2,1)S(1)} %get-tuple-element.17._.own), channel_id=1, source_target_pairs={{0,4},{1,5},{2,6},{3,7},{4,0},{5,1},{6,2},{7,3},{8,12},{9,13},{10,... | collective-permute-start | bytes 98312 | tf_op jit(solution)/shard_map/ppermute | solution.py:384
  31.6 2.9 %perturb.1 = (f32[8,512,128]{2,1,0:T(8,128)S(1)}, bf16[128,1024]{1,0:T(8,128)(2,1)S(1)}) custom-call(s32[9]{0:T(128)S(1)} %pad_add_fusion.scal, bf16[8,512,128]{2,1,0:T(8,128)(2,1)S(1)} %copy-done.1, bf16[128,128]{1,0:T(8,128)(2,1)S(1)} %collective-permute-done.even, bf16[128,128]{1,0:T(8,128)(2,1)S(1)} %collective-permute-done.1.odd, ...), custom_call_target="tpu_custom_call" | custom-call | flops 134217728 | bytes 4194304 | tf_op jit(solution)/shard_map/perturb/pallas_call | solution.py:432
  34.6 3.8 %down.1 = (bf16[8,512,128]{2,1,0:T(8,128)(2,1)}, f32[1,8]{1,0:T(1,128)}) custom-call(s32[9]{0:T(128)S(1)} %pad_add_fusion.scal, bf16[128,1024]{1,0:T(8,128)(2,1)S(1)} %get-tuple-element.18.final_map, bf16[128,128]{1,0:T(8,128)(2,1)S(1)} %get-tuple-element.17._.own, bf16[128,128]{1,0:T(8,128)(2,1)S(1)} %collective-permute-done.5.refs_0_, ...), custom_call_target="tpu_custom_call" | custom-call | flops 536870912 | bytes 8388608 | tf_op jit(solution)/shard_map/down/pallas_call | solution.py:465
  (36 shorter events, 0.1 us)
Async XLA Ops:
  1.4 1.2 %copy-start = (bf16[8,512,128]{2,1,0:T(8,128)(2,1)S(1)}, bf16[8,512,128]{2,1,0:T(8,128)(2,1)}, u32[]{:S(2)}) copy-start(bf16[8,512,128]{2,1,0:T(8,128)(2,1)} %forward.3) | copy-start | bytes 3145732
  6.0 13.1 %copy-start.3 = (bf16[8,512,128]{2,1,0:T(8,128)(2,1)S(1)}, bf16[8,512,128]{2,1,0:T(8,128)(2,1)}, u32[]{:S(2)}) copy-start(bf16[8,512,128]{2,1,0:T(8,128)(2,1)} %source.3) | copy-start | bytes 3145732
  6.0 13.1 %copy-start.4 = (bf16[4,2,256,256]{3,2,1,0:T(8,128)(2,1)S(1)}, bf16[4,2,256,256]{3,2,1,0:T(8,128)(2,1)}, u32[]{:S(2)}) copy-start(bf16[4,2,256,256]{3,2,1,0:T(8,128)(2,1)} %down_ref.3) | copy-start | bytes 3145732
  6.0 13.1 %copy-start.9 = (bf16[4,2,128,256]{3,2,1,0:T(8,128)(2,1)S(1)}, bf16[4,2,128,256]{3,2,1,0:T(8,128)(2,1)}, u32[]{:S(2)}) copy-start(bf16[4,2,128,256]{3,2,1,0:T(8,128)(2,1)} %up_ref.3) | copy-start | bytes 1572868
  6.0 13.1 %copy-start.10 = (bf16[4,2,256,128]{3,2,1,0:T(8,128)(2,1)S(1)}, bf16[4,2,256,128]{3,2,1,0:T(8,128)(2,1)}, u32[]{:S(2)}) copy-start(bf16[4,2,256,128]{3,2,1,0:T(8,128)(2,1)} %parent_ref.3) | copy-start | bytes 1572868
  10.9 15.2 %collective-permute-start.4 = (bf16[128,128]{1,0:T(8,128)(2,1)S(1)}, bf16[128,128]{1,0:T(8,128)(2,1)S(1)}, u32[]{:S(2)}, u32[]{:S(2)}) collective-permute-start(bf16[128,128]{1,0:T(8,128)(2,1)S(1)} %get-tuple-element.15._.own), channel_id=1, source_target_pairs={{0,3},{1,2},{2,1},{3,0},{4,7},{5,6},{6,5},{7,4},{8,11},{9,10},{10,... | collective-permute-start | bytes 98312 | tf_op jit(solution)/shard_map/ppermute | solution.py:384
  13.4 12.7 %collective-permute-start.3 = (bf16[128,128]{1,0:T(8,128)(2,1)S(1)}, bf16[128,128]{1,0:T(8,128)(2,1)S(1)}, u32[]{:S(2)}, u32[]{:S(2)}) collective-permute-start(bf16[128,128]{1,0:T(8,128)(2,1)S(1)} %get-tuple-element.15._.own), channel_id=1, source_target_pairs={{0,2},{1,3},{2,0},{3,1},{4,6},{5,7},{6,4},{7,5},{8,10},{9,11},{10,... | collective-permute-start | bytes 98312 | tf_op jit(solution)/shard_map/ppermute | solution.py:384
  14.0 12.1 %collective-permute-start.2 = (bf16[128,128]{1,0:T(8,128)(2,1)S(1)}, bf16[128,128]{1,0:T(8,128)(2,1)S(1)}, u32[]{:S(2)}, u32[]{:S(2)}) collective-permute-start(bf16[128,128]{1,0:T(8,128)(2,1)S(1)} %get-tuple-element.15._.own), channel_id=1, source_target_pairs={{0,1},{1,0},{2,3},{3,2},{4,5},{5,4},{6,7},{7,6},{8,9},{9,8},{10,11... | collective-permute-start | bytes 98312 | tf_op jit(solution)/shard_map/ppermute | solution.py:384
  14.0 17.5 %collective-permute-start = (bf16[128,128]{1,0:T(8,128)(2,1)S(1)}, bf16[128,128]{1,0:T(8,128)(2,1)S(1)}, u32[]{:S(2)}, u32[]{:S(2)}) collective-permute-start(bf16[128,128]{1,0:T(8,128)(2,1)S(1)} %get-tuple-element.13), channel_id=1, source_target_pairs={{0,1},{1,0},{2,3},{3,2},{4,5},{5,4},{6,7},{7,6},{8,9},{9,8},{10,11... | collective-permute-start | bytes 98312 | tf_op jit(solution)/shard_map/ppermute | solution.py:384
  14.5 17.0 %copy-start.1 = (bf16[8,512,128]{2,1,0:T(8,128)(2,1)S(1)}, bf16[8,512,128]{2,1,0:T(8,128)(2,1)}, u32[]{:S(2)}) copy-start(bf16[8,512,128]{2,1,0:T(8,128)(2,1)} %forward.3) | copy-start | bytes 3145732
  14.5 17.0 %copy-start.11 = (bf16[3,2,128,128]{3,2,1,0:T(8,128)(2,1)S(1)}, bf16[3,2,128,128]{3,2,1,0:T(8,128)(2,1)}, u32[]{:S(2)}) copy-start(bf16[3,2,128,128]{3,2,1,0:T(8,128)(2,1)} %rim_left.1) | copy-start | bytes 589828
  14.5 17.0 %copy-start.12 = (bf16[3,2,128,128]{3,2,1,0:T(8,128)(2,1)S(1)}, bf16[3,2,128,128]{3,2,1,0:T(8,128)(2,1)}, u32[]{:S(2)}) copy-start(bf16[3,2,128,128]{3,2,1,0:T(8,128)(2,1)} %rim_right.1) | copy-start | bytes 589828
  14.5 17.0 %copy-start.13 = (bf16[2,128,128]{2,1,0:T(8,128)(2,1)S(1)}, bf16[2,128,128]{2,1,0:T(8,128)(2,1)}, u32[]{:S(2)}) copy-start(bf16[2,128,128]{2,1,0:T(8,128)(2,1)} %root_ref.1) | copy-start | bytes 196612
  14.5 17.0 %copy-start.14 = (f32[3,2,512]{2,1,0:T(2,128)S(1)}, f32[3,2,512]{2,1,0:T(2,128)}, u32[]{:S(2)}) copy-start(f32[3,2,512]{2,1,0:T(2,128)} %shape_ref.1) | copy-start | bytes 36868
  14.5 17.0 %copy-start.15 = (f32[128]{0:T(128)S(1)}, f32[128]{0:T(128)}, u32[]{:S(2)}) copy-start(f32[128]{0:T(128)} %param.33) | copy-start | bytes 1540
  14.5 17.0 %copy-start.16 = (f32[128]{0:T(128)S(1)}, f32[128]{0:T(128)}, u32[]{:S(2)}) copy-start(f32[128]{0:T(128)} %param.34) | copy-start | bytes 1540
  14.6 17.0 %copy-start.17 = (s32[64]{0:T(128)S(1)}, s32[64]{0:T(128)}, u32[]{:S(2)}) copy-start(s32[64]{0:T(128)} %param.35) | copy-start | bytes 772
  14.6 16.9 %collective-permute-start.1 = (bf16[128,128]{1,0:T(8,128)(2,1)S(1)}, bf16[128,128]{1,0:T(8,128)(2,1)S(1)}, u32[]{:S(2)}, u32[]{:S(2)}) collective-permute-start(bf16[128,128]{1,0:T(8,128)(2,1)S(1)} %get-tuple-element.14), channel_id=1, source_target_pairs={{0,15},{1,2},{2,1},{3,4},{4,3},{5,6},{6,5},{7,8},{8,7},{9,10},{10,... | collective-permute-start | bytes 98312 | tf_op jit(solution)/shard_map/ppermute | solution.py:391
  19.1 1.9 %copy-start.18 = (bf16[3,2,512,512]{3,2,1,0:T(8,128)(2,1)S(1)}, bf16[3,2,512,512]{3,2,1,0:T(8,128)(2,1)}, u32[]{:S(2)}) copy-start(bf16[3,2,512,512]{3,2,1,0:T(8,128)(2,1)} %solve.1) | copy-start | bytes 9437188
  26.1 8.4 %copy-start.5 = (bf16[3,2,512,128]{3,2,1,0:T(8,128)(2,1)S(1)}, bf16[3,2,512,128]{3,2,1,0:T(8,128)(2,1)}, u32[]{:S(2)}) copy-start(bf16[3,2,512,128]{3,2,1,0:T(8,128)(2,1)} %refs_5_.1) | copy-start | bytes 2359300
  26.1 8.4 %copy-start.7 = (bf16[8,2,128,128]{3,2,1,0:T(8,128)(2,1)S(1)}, bf16[8,2,128,128]{3,2,1,0:T(8,128)(2,1)}, u32[]{:S(2)}) copy-start(bf16[8,2,128,128]{3,2,1,0:T(8,128)(2,1)} %refs_4_.1) | copy-start | bytes 1572868
  27.1 7.5 %collective-permute-start.7 = (bf16[128,128]{1,0:T(8,128)(2,1)S(1)}, bf16[128,128]{1,0:T(8,128)(2,1)S(1)}, u32[]{:S(2)}, u32[]{:S(2)}) collective-permute-start(bf16[128,128]{1,0:T(8,128)(2,1)S(1)} %get-tuple-element.17._.own), channel_id=1, source_target_pairs={{0,12},{1,13},{2,14},{3,15},{4,8},{5,9},{6,10},{7,11},{8,4},{9,5},... | collective-permute-start | bytes 98312 | tf_op jit(solution)/shard_map/ppermute | solution.py:384
  27.6 6.9 %collective-permute-start.6 = (bf16[128,128]{1,0:T(8,128)(2,1)S(1)}, bf16[128,128]{1,0:T(8,128)(2,1)S(1)}, u32[]{:S(2)}, u32[]{:S(2)}) collective-permute-start(bf16[128,128]{1,0:T(8,128)(2,1)S(1)} %get-tuple-element.17._.own), channel_id=1, source_target_pairs={{0,8},{1,9},{2,10},{3,11},{4,12},{5,13},{6,14},{7,15},{8,0},{9,1},... | collective-permute-start | bytes 98312 | tf_op jit(solution)/shard_map/ppermute | solution.py:384
  27.6 7.0 %collective-permute-start.5 = (bf16[128,128]{1,0:T(8,128)(2,1)S(1)}, bf16[128,128]{1,0:T(8,128)(2,1)S(1)}, u32[]{:S(2)}, u32[]{:S(2)}) collective-permute-start(bf16[128,128]{1,0:T(8,128)(2,1)S(1)} %get-tuple-element.17._.own), channel_id=1, source_target_pairs={{0,4},{1,5},{2,6},{3,7},{4,0},{5,1},{6,2},{7,3},{8,12},{9,13},{10,... | collective-permute-start | bytes 98312 | tf_op jit(solution)/shard_map/ppermute | solution.py:384
  (3 other events, 3.4 us)

commit v2 on v1

v2 whole, which is shorter than its diff:
```python
import functools
import math

import jax
import jax.numpy as jnp
from jax import lax
from jax.experimental import pallas as pl
from jax.experimental.pallas import tpu as pltpu
from jax.sharding import PartitionSpec as P

F32 = jnp.float32
BF16 = jnp.bfloat16
MIB = 1 << 20
VM = pl.BlockSpec(memory_space=pltpu.VMEM)
HBM = pl.BlockSpec(memory_space=pltpu.HBM)


def params(mib):
    return pltpu.CompilerParams(vmem_limit_bytes=mib * MIB)


def cost(flops, nbytes):
    return pl.CostEstimate(flops=flops, bytes_accessed=nbytes, transcendentals=0)


def half_sign(width):
    lane = lax.broadcasted_iota(jnp.int32, (1, width), 1)
    return jnp.where(lane < width // 2, -1.0, 1.0).astype(F32)


def turn(values):
    width = values.shape[-1]
    return pltpu.roll(values, width // 2, 1) * half_sign(width)


def dot(a, b):
    return jnp.dot(a, b, preferred_element_type=F32)


def split(x):
    high = x.astype(BF16)
    return high, (x - high.astype(F32)).astype(BF16)


def embed(re, im):
    return jnp.concatenate(
        [jnp.concatenate([re, -im], axis=1), jnp.concatenate([im, re], axis=1)], axis=0
    )


def times(re, im, stacked):
    left = embed(re, im)
    if stacked.dtype == BF16:
        return dot(left, stacked)
    high, low = split(stacked)
    return dot(left, high) + dot(left, low)


def side_by_side(stacked):
    rows = stacked.shape[0] // 2
    return jnp.concatenate([stacked[:rows], stacked[rows:]], axis=1)


def groups_of(levels):
    return [tuple(range(low, min(low + 2, levels))) for low in range(0, levels, 2)]


def wide(ref, *at):
    return jnp.concatenate([ref[(*at, 0)], ref[(*at, 1)]], axis=1)


def tall(ref, *at):
    return jnp.concatenate([ref[(*at, 0)], ref[(*at, 1)]], axis=0)


def rows_of(ref, level, bit):
    rank = ref.shape[2] // 2
    start = pl.multiple_of(bit * rank, rank)
    return ref[level, 0, pl.ds(start, rank), :], ref[level, 1, pl.ds(start, rank), :]


def turned(value):
    return turn(value.astype(F32)).astype(BF16)


def slot_count(cells, classes):
    return (cells + classes) // 2


def table_size(slots):
    return -(-(3 * slots + 3) // 128) * 128


class Pairs:
    def __init__(self, table, slots):
        self.table, self.slots = table, slots

    def ends(self):
        return self.table[3 * self.slots + 1], self.table[3 * self.slots + 2]

    def __getitem__(self, slot):
        return tuple(self.table[i * self.slots + slot] for i in range(3))

    def used(self):
        return self.table[3 * self.slots]


def fill_pairs(scal, table, cells, classes):
    slots = slot_count(cells, classes)
    slot = jnp.int32(0)
    for k in range(classes):
        half = jnp.int32(0)
        for p in range(cells):
            mine = scal[p] == k

            @pl.when(jnp.logical_and(mine, half == 0))
            def _first(k=k, p=p, slot=slot):
                table[slot] = k
                table[slots + slot] = p

            @pl.when(mine)
            def _second(p=p, slot=slot):
                table[2 * slots + slot] = p

            step = mine.astype(jnp.int32)
            slot = slot + step * half
            half = jnp.where(mine, 1 - half, half)
        slot = slot + half
    table[3 * slots] = slot
    table[3 * slots + 1] = scal[0]
    table[3 * slots + 2] = scal[cells - 1]
    for s in range((cells + 1) // 2, slots):

        @pl.when(s >= slot)
        def _spare(s=s):
            for i in range(3):
                table[i * slots + s] = table[i * slots]


def up_kernel(
    classes_h,
    source,
    skeleton,
    merge,
    forward,
    out,
    joint,
    odd,
    table_out,
    scal,
    table,
    src_v,
    skel_v,
    merge_v,
    cell_v,
    sems,
):
    cells, nodes, width = src_v.shape
    classes = skel_v.shape[0]
    rank = skel_v.shape[2]
    rim = odd.shape[0]
    parity = lax.axis_index("loop") & 1
    copies = []

    def start(src, dst, i):
        c = pltpu.make_async_copy(src, dst, sems.at[i])
        c.start()
        copies.append(c)

    start(classes_h, scal, 0)
    start(skeleton, skel_v, 1)
    start(source, src_v, 2)
    start(merge, merge_v, 3)
    last = (cells - 1, nodes - rim)
    even_cell = jnp.where(parity == 0, last[0], 0)
    even_row = pl.multiple_of(jnp.where(parity == 0, last[1], 0), rim)
    odd_cell = jnp.where(parity == 1, last[0], 0)
    odd_row = pl.multiple_of(jnp.where(parity == 1, last[1], 0), rim)
    start(forward.at[even_cell, pl.ds(even_row, rim), :], joint.at[pl.ds(rank, rim), :], 4)
    start(forward.at[odd_cell, pl.ds(odd_row, rim), :], odd, 5)
    copies[0].wait()
    fill_pairs(scal, table, cells, classes)
    start(table, table_out, 6)
    slots = slot_count(cells, classes)
    pairs = Pairs(table, slots)
    copies[1].wait()
    copies[2].wait()
    for s in range(slots):
        k, a, b = pairs[s]
        both = dot(tall(skel_v, k), jnp.concatenate([src_v[a], src_v[b]], axis=1))
        for i, p in enumerate((a, b)):
            part = both[:, i * width : (i + 1) * width]
            cell_v[p] = (part[:rank] + turn(part[rank:])).astype(BF16)
    copies[3].wait()
    total = None
    for p in range(0, cells, 2):
        mine = range(p, min(p + 2, cells))
        left = jnp.concatenate(
            [jnp.concatenate([merge_v[i, part] for i in mine], axis=1) for part in range(2)], axis=0
        )
        term = dot(left, jnp.concatenate([cell_v[i] for i in mine], axis=0))
        total = term if total is None else total + term
    block = (total[:rank] + turn(total[rank:])).astype(BF16)
    out[...] = block
    joint[:rank, :] = block
    for c in copies[4:]:
        c.wait()


def fetch_table(table_v, table, sem):
    copy = pltpu.make_async_copy(table_v, table, sem.at[0])
    copy.start()
    return copy


def local_kernel(
    table_v, source, solve, down_ref, parent_ref, _, local, maps, table, table_sem, *, groups
):
    fetched = fetch_table(table_v, table, table_sem)
    cells, nodes, width = source.shape
    position = lax.axis_index("loop")
    for g, group in enumerate(groups[:-1]):
        if len(group) == 2:
            low, high = group
            re, im = rows_of(parent_ref, low, (position >> low) & 1)
            inner = jnp.concatenate(rows_of(down_ref, high, (position >> high) & 1), axis=0)
            maps[g] = jnp.concatenate(split(side_by_side(times(re, im, inner))), axis=0)
    slots = slot_count(cells, solve.shape[0])
    fetched.wait()
    pairs = Pairs(table, slots)
    for s in range(slots):
        k, a, b = pairs[s]
        va, vb = source[a], source[b]
        right = jnp.concatenate(
            [
                jnp.concatenate([va, vb], axis=1),
                jnp.concatenate([turned(va), turned(vb)], axis=1),
            ],
            axis=0,
        )
        value = dot(wide(solve, k), right)
        local[a] = value[:, :width]
        local[b] = value[:, width:]


def gather_nodes(group, position, own, arrived, nodes_v):
    count = 1 << len(group)
    index = (position >> group[0]) & (count - 1)
    rank = own.shape[0]
    for mask in range(count):
        value = own[...] if mask == 0 else arrived[mask - 1][:rank, :]
        where = index ^ mask
        nodes_v[where] = value
        nodes_v[count + where] = turned(value)


def pair_stack(nodes_v, count, first):
    return jnp.concatenate(
        [nodes_v[first], nodes_v[first + 1], nodes_v[count + first], nodes_v[count + first + 1]],
        axis=0,
    )


def middle_stack(group, nodes_v, up_ref):
    both = jnp.concatenate([pair_stack(nodes_v, 4, 0), pair_stack(nodes_v, 4, 2)], axis=1)
    y = dot(wide(up_ref, group[0]), both)
    width = y.shape[1] // 2
    parts = [y[:, :width], y[:, width:]]
    return split(jnp.concatenate(parts + [turn(p) for p in parts], axis=0))


def combine_kernel(maps, up_ref, down_ref, own, *refs, group, index):
    count = 1 << len(group)
    arrived = refs[: count - 1]
    node, part, nodes_v = refs[count - 1 :]
    position = lax.axis_index("loop")
    gather_nodes(group, position, own, arrived, nodes_v)
    low_down = jnp.concatenate(rows_of(down_ref, group[0], (position >> group[0]) & 1), axis=1)
    if len(group) == 1:
        stack = pair_stack(nodes_v, 2, 0)
        node[...] = dot(wide(up_ref, group[0]), stack).astype(BF16)
        part[...] = dot(low_down, stack)
        return
    high, low = middle_stack(group, nodes_v, up_ref)
    rank = own.shape[0]
    up = wide(up_ref, group[1])
    node[...] = (dot(up, high) + dot(up, low)).astype(BF16)
    mine = pair_stack(nodes_v, 4, 2 * ((position >> group[1]) & 1))
    map_high, map_low = maps[index, :rank], maps[index, rank:]
    part[...] = (
        dot(map_high, high) + dot(map_high, low) + dot(map_low, high) + dot(low_down, mine)
    )


def perturb_kernel(
    table_v,
    forward,
    joint,
    odd,
    rim_left,
    rim_right,
    shape_ref,
    angle_ref,
    weight_ref,
    ids_ref,
    up_ref,
    down_ref,
    parent_ref,
    root_ref,
    _,
    weighted,
    final_map,
    columns,
    table,
    table_sem,
    *,
    groups,
    device_count,
):
    fetched = fetch_table(table_v, table, table_sem)
    cells, nodes, width = forward.shape
    rim = odd.shape[0]
    classes = shape_ref.shape[0]
    position = lax.axis_index("loop")
    parity = position & 1

    group = groups[-1]
    top = group[-1]
    total = times(root_ref[0], root_ref[1], tall(up_ref, top))
    for level in reversed(group):
        bit = (position >> level) & 1
        re, im = rows_of(parent_ref, level, bit)
        total = times(re, im, total)
        down = jnp.concatenate(rows_of(down_ref, level, bit), axis=0).astype(F32)
        if level == top:
            total = total + down
        else:
            total = jnp.concatenate([total, down], axis=1)
    for lower in reversed(groups[:-1]):
        for level in reversed(lower):
            re, im = rows_of(parent_ref, level, (position >> level) & 1)
            total = times(re, im, total)
    pieces = [total[:, c : c + down.shape[1]] for c in range(0, total.shape[1], down.shape[1])]
    whole = jnp.concatenate([side_by_side(p) for p in pieces], axis=1)
    final_map[...] = jnp.concatenate(split(whole), axis=0)

    ids = jnp.concatenate([ids_ref[...], ids_ref[...]], axis=1)
    entries = angle_ref.shape[1]
    chosen = lax.broadcasted_iota(jnp.int32, (entries, width), 0) == ids

    def looked_up(row):
        column = jnp.transpose(jnp.broadcast_to(row, (8, entries)))[:, :1]
        return jnp.sum(jnp.where(chosen, column, 0.0), axis=0, keepdims=True)

    scale = half_sign(width) * (-1.0 / math.sqrt(nodes * (width // 2)))
    weights = looked_up(weight_ref[...]) * scale
    for k in range(classes):
        flipped = jnp.transpose(jnp.concatenate([shape_ref[k]] * 4, axis=0))
        columns[k, 0] = jnp.broadcast_to(flipped[:, 0:1], (nodes, width)) * weights
        columns[k, 1] = jnp.broadcast_to(flipped[:, 1:2], (nodes, width)) * weights

    even = joint[joint.shape[0] - rim :, :]
    before = jnp.where(parity == 1, even, odd[...])
    after = jnp.where(parity == 0, even, odd[...])

    def left_input(p):
        return jnp.where(p == 0, before, forward[jnp.maximum(p - 1, 0), nodes - rim :, :])

    def right_input(p):
        return jnp.where(p == cells - 1, after, forward[jnp.minimum(p + 1, cells - 1), :rim, :])

    def stacked(values):
        return jnp.concatenate(
            [
                jnp.concatenate(values, axis=1),
                jnp.concatenate([turned(v) for v in values], axis=1),
            ],
            axis=0,
        )

    slots = slot_count(cells, classes)
    pairs = Pairs(table, slots)
    fetched.wait()
    for s in range(slots):
        k, a, b = pairs[s]
        left = dot(wide(rim_left, k), stacked([left_input(a), left_input(b)]))
        right = dot(wide(rim_right, k), stacked([right_input(a), right_input(b)]))
        for i, p in enumerate((a, b)):
            field = forward[p].astype(F32)
            value = columns[k, 0] * field + columns[k, 1] * turn(field)
            lanes = slice(i * width, (i + 1) * width)
            weighted[p, :rim, :] = value[:rim] + left[:, lanes] * weights
            weighted[p, rim : nodes - rim, :] = value[rim : nodes - rim]
            weighted[p, nodes - rim :, :] = value[nodes - rim :] + right[:, lanes] * weights

    def seam(ref, k, block, sign):
        angles = looked_up(angle_ref[...])
        term = dot(wide(ref, k), jnp.concatenate([block, turned(block)], axis=0))
        turned_term = term * jnp.cos(angles) + turn(term) * (jnp.sin(angles) * sign)
        return (turned_term - term) * weights

    ends = pairs.ends()

    @pl.when(position == 0)
    def _first():
        weighted[0, :rim, :] += seam(rim_left, ends[0], before, -1.0)

    @pl.when(position == device_count - 1)
    def _last():
        weighted[cells - 1, nodes - rim :, :] += seam(rim_right, ends[1], after, 1.0)


def down_kernel(table_v, final_map, up_ref, own, *refs, group):
    count = 1 << len(group)
    arrived = refs[: count - 1]
    part, split_ref, lift, local, weighted, adjoint, gradient = refs[count - 1 : count + 6]
    nodes_v, cell_v, out_v, sums, sems, table, table_sem = refs[count + 6 :]
    fetched = fetch_table(table_v, table, table_sem)
    rank = own.shape[0]
    cells, nodes, width = local.shape
    position = lax.axis_index("loop")
    gather_nodes(group, position, own, arrived, nodes_v)
    map_high, map_low = final_map[:rank], final_map[rank:]
    if len(group) == 1:
        stack = pair_stack(nodes_v, 2, 0)
        field = dot(map_high, stack) + dot(map_low, stack)
    else:
        high, low = middle_stack(group, nodes_v, up_ref)
        mine = pair_stack(nodes_v, 4, 2 * ((position >> group[1]) & 1))
        stack = jnp.concatenate([high, mine], axis=0)
        field = dot(map_high, stack) + dot(map_low, stack) + dot(map_high[:, : low.shape[0]], low)
    field = field + part[...]
    both = jnp.concatenate([field.astype(BF16), turn(field).astype(BF16)], axis=0)
    for p in range(cells):
        cell = dot(wide(split_ref, p), both)
        cell_v[p] = jnp.concatenate([cell.astype(BF16), turn(cell).astype(BF16)], axis=0)

    slots = slot_count(cells, lift.shape[0])
    pairs = Pairs(table, slots)
    fetched.wait()

    def send(p):
        return pltpu.make_async_copy(out_v.at[p], adjoint.at[p], sems.at[p])

    def lift_pair(s):
        k, a, b = pairs[s]
        value = dot(wide(lift, k), jnp.concatenate([cell_v[a], cell_v[b]], axis=1))
        for i, p in enumerate((a, b)):
            rounded = (local[p] + value[:, i * width : (i + 1) * width]).astype(BF16)
            out_v[p] = rounded
            total = jnp.sum(rounded.astype(F32) * weighted[p], axis=0, keepdims=True)
            sums[p] = jnp.broadcast_to(total, (8, width))
        send(a).start()

        @pl.when(a != b)
        def _():
            send(b).start()

    for s in range(slots):
        if s < (cells + 1) // 2:
            lift_pair(s)
        else:
            pl.when(s < pairs.used())(functools.partial(lift_pair, s))

    rows = jnp.concatenate([sums[p, :1] for p in range(cells)], axis=0)
    row = lax.broadcasted_iota(jnp.int32, (cells, cells), 0)
    lane = lax.broadcasted_iota(jnp.int32, (cells, cells), 1)
    across = jnp.sum(rows, axis=1, keepdims=True)
    gradient[...] = jnp.sum(jnp.where(row == lane, across, 0.0), axis=0, keepdims=True)
    for p in range(cells):
        send(p).wait()


def shards(
    classes,
    forward_field,
    adjoint_source,
    leaf_solve,
    leaf_lift,
    leaf_skeleton,
    block_merge,
    block_split,
    level_up,
    level_down,
    level_parent,
    root_solve,
    rim_left,
    rim_right,
    shape_derivative,
    illum_angle,
    illum_weight,
    illum_ids,
):
    position = lax.axis_index("loop")
    device_count = lax.axis_size("loop")
    cells, nodes, width = adjoint_source.shape
    class_count = leaf_solve.shape[0]
    rank = root_solve.shape[-1]
    rim = rim_left.shape[-1]
    levels = level_up.shape[0]
    groups = groups_of(levels)
    slots = slot_count(cells, class_count)
    sds = jax.ShapeDtypeStruct
    node = sds((rank, width), BF16)
    halo = sds((rim, width), BF16)

    size = table_size(slots)
    table_scratch = [pltpu.SMEM((size,), jnp.int32), pltpu.SemaphoreType.DMA((1,))]
    pinned = functools.partial(pltpu.with_memory_space_constraint, memory_space=pltpu.HBM)
    source, joint, odd, table = pl.pallas_call(
        up_kernel,
        out_shape=(node, sds((rank + rim, width), BF16), halo, sds((size,), jnp.int32)),
        in_specs=[HBM] * 5,
        out_specs=(VM, VM, VM, VM),
        scratch_shapes=[
            pltpu.SMEM((cells,), jnp.int32),
            pltpu.SMEM((size,), jnp.int32),
            pltpu.VMEM((cells, nodes, width), BF16),
            pltpu.VMEM((class_count, 2, rank, nodes), BF16),
            pltpu.VMEM(block_merge.shape, BF16),
            pltpu.VMEM((cells, rank, width), BF16),
            pltpu.SemaphoreType.DMA((7,)),
        ],
        compiler_params=params(8),
        cost_estimate=cost(64 * cells * rank * nodes * width, 64 * MIB),
        name="up",
    )(*map(pinned, (classes, adjoint_source, leaf_skeleton, block_merge, forward_field)))

    def exchange(value, mask):
        pairs = [(i, i ^ mask) for i in range(device_count)]
        return lax.ppermute(value, "loop", pairs)

    def odd_exchange(value):
        pairs = [
            (i, (i + 1) % device_count if i % 2 else (i - 1) % device_count)
            for i in range(device_count)
        ]
        return lax.ppermute(value, "loop", pairs)

    def gather(value, group):
        base = 1 << group[0]
        return [exchange(value, base * m) for m in range(1, 1 << len(group))]

    odd_in = odd_exchange(odd)
    arrived = [exchange(joint, 1)] + [
        exchange(source, m) for m in range(2, 1 << len(groups[0]))
    ]
    joint_in = arrived[0]

    local, maps = pl.pallas_call(
        functools.partial(local_kernel, groups=groups),
        out_shape=(
            sds((cells, nodes, width), F32),
            sds((max(len(groups) - 1, 1), 2 * rank, 4 * rank), BF16),
        ),
        in_specs=[VM] * 6,
        out_specs=(VM, VM),
        scratch_shapes=table_scratch,
        compiler_params=params(4),
        cost_estimate=cost(8 * cells * nodes * nodes * width, 6 * MIB),
        name="local",
    )(table, adjoint_source, leaf_solve, level_down, level_parent, source)

    own = source
    fields = []
    for g, group in enumerate(groups[:-1]):
        count = 1 << len(group)
        own, part = pl.pallas_call(
            functools.partial(combine_kernel, group=group, index=g),
            out_shape=(node, sds((rank, width), F32)),
            in_specs=[VM] * (3 + count),
            out_specs=(VM, VM),
            scratch_shapes=[pltpu.VMEM((2 * count, rank, width), BF16)],
            compiler_params=params(4),
            cost_estimate=cost(16 * rank * rank * width, MIB),
            name="combine",
        )(maps, level_up, level_down, own, *arrived)
        fields.append((group, part))
        arrived = gather(own, groups[g + 1])

    group = groups[-1]
    count = 1 << len(group)
    weighted, final_map = pl.pallas_call(
        functools.partial(perturb_kernel, groups=groups, device_count=device_count),
        out_shape=(
            sds((cells, nodes, width), F32),
            sds((2 * rank, 2 * (rank << len(group))), BF16),
        ),
        in_specs=[VM] * 15,
        out_specs=(VM, VM),
        scratch_shapes=[pltpu.VMEM((class_count, 2, nodes, width), F32)] + table_scratch,
        compiler_params=params(8),
        cost_estimate=cost(8 * cells * rim * rim * width, 4 * MIB),
        name="perturb",
    )(
        table,
        forward_field,
        joint_in,
        odd_in,
        rim_left,
        rim_right,
        shape_derivative,
        illum_angle[None],
        illum_weight[None],
        illum_ids[None],
        level_up,
        level_down,
        level_parent,
        root_solve,
        own,
    )

    part = fold_parts(fields, level_parent, position, rank, width)
    adjoint, gradient = pl.pallas_call(
        functools.partial(down_kernel, group=group),
        out_shape=(sds((cells, nodes, width), BF16), sds((1, cells), F32)),
        in_specs=[VM] * (count + 3 + 5),
        out_specs=(HBM, VM),
        scratch_shapes=[
            pltpu.VMEM((2 * count, rank, width), BF16),
            pltpu.VMEM((cells, 2 * rank, width), BF16),
            pltpu.VMEM((cells, nodes, width), BF16),
            pltpu.VMEM((cells, 8, width), F32),
            pltpu.SemaphoreType.DMA((cells,)),
        ]
        + table_scratch,
        compiler_params=params(6),
        cost_estimate=cost(8 * cells * nodes * rank * width, 8 * MIB),
        name="down",
    )(table, final_map, level_up, own, *arrived, part, block_split, leaf_lift, local, weighted)
    return adjoint, gradient[0]


def fold_parts(fields, level_parent, position, rank, width):
    if not fields:
        return jnp.zeros((rank, width), F32)
    total = fields[-1][1]
    for group, part in reversed(fields[:-1]):
        for level in reversed(group):
            start = ((position >> level) & 1) * rank
            rows = lax.dynamic_slice_in_dim(level_parent[level], start, rank, 1).astype(F32)
            direct = jnp.dot(rows[0], total, precision=lax.Precision.HIGHEST)
            twisted = jnp.dot(rows[1], total, precision=lax.Precision.HIGHEST)
            half = width // 2
            total = direct + jnp.concatenate([-twisted[:, half:], twisted[:, :half]], axis=1)
        total = total + part
    return total


def solution(mesh):
    return jax.shard_map(
        shards,
        mesh=mesh,
        in_specs=(
            P(("parts", "loop")),
            P(("parts", "loop"), None, None),
            P(("parts", "loop"), None, None),
            P("parts", None, None, None),
            P("parts", None, None, None),
            P("parts", None, None, None),
            P("parts", None, None, None),
            P("parts", None, None, None),
            P("parts", None, None, None),
            P("parts", None, None, None),
            P("parts", None, None, None),
            P("parts", None, None),
            P("parts", None, None, None),
            P("parts", None, None, None),
            P("parts", None, None),
            P("parts"),
            P("parts"),
            P(),
        ),
        out_specs=(P(("parts", "loop"), None, None), P(("parts", "loop"))),
        check_vma=False,
    )
```

time: 38.7 us -> 25.2 us (0.65)
  local copies, waits for them, and re-layouts: 6.57 us -> 0.09 us
  Pallas kernels: 17.6 us -> 12 us
  other arithmetic: 0.73 us -> 0 us
  starting transfers between devices: 12.6 us -> 12 us
    unnamed x38 -> x30, local copies, waits for them, and re-layouts: 6.57 us -> 0.09 us
    pallas_call x1, Pallas kernels: 5.09 us -> 2.28 us  [shards(): pl.pallas_call(functools.partial(local_kernel, groups=groups), out_shape=...]
    pallas_call x3, Pallas kernels: 9.61 us -> 6.88 us  [the longest x1 3.37 us: shards(): pl.pallas_call(functools.partial(down_kernel, group=group), out_shape=(sd...]
    concatenate x1 -> x0, other arithmetic: 0.73 us -> none  [shards(): scal = jnp.concatenate([classes, position.astype(jnp.int32)[None]])]
    ppermute x7 -> x6, starting transfers between devices: 8.1 us -> 7.6 us  [exchange(): return lax.ppermute(value, 'loop', pairs)]
  transfers between devices with their start and end apart: 8 -> 7, of which waited for: 0 -> 0; matrix products, arithmetic and copies ran while one was open for 0% -> 0% of each run, Pallas kernels for 23% -> 23%
where the time goes in v2:
time: 25.2 us; the launch traced here: 25 us
  Pallas kernels  12 us (48%)
  starting transfers between devices  12 us (48%)
  between operations  0.92 us (4%)
    ppermute x6, starting transfers between devices, exchange(): return lax.ppermute(value, 'loop', pairs)  7.6 us
    ppermute x1, starting transfers between devices, odd_exchange(): return lax.ppermute(value, 'loop', pairs)  4.42 us
    pallas_call x1, Pallas kernels, shards(): pl.pallas_call(functools.partial(down_kernel, group=group), out_shape=(sd...  3.37 us
    pallas_call x1, Pallas kernels, shards(): pl.pallas_call(functools.partial(perturb_kernel, groups=groups, device_co...  2.81 us
    pallas_call x1, Pallas kernels, shards(): pl.pallas_call(up_kernel, out_shape=(node, sds((rank + rim, width), BF16)...  2.76 us
    pallas_call x1, Pallas kernels, shards(): pl.pallas_call(functools.partial(local_kernel, groups=groups), out_shape=...  2.28 us
    pallas_call x1, Pallas kernels, shards(): pl.pallas_call(functools.partial(combine_kernel, group=group, index=g), o...  0.75 us
  transfers between devices with their start and end apart: 7, of which 0 were waited for; matrix products, arithmetic and copies ran while one was open for 0% of the time, Pallas kernels for 23%

profile of v2, /device:TPU:0, one launch (start us, length us, event | category | flops | bytes accessed | tf_op | source)
XLA Modules:
  0.0 25.0 jit_solution(13445941149447303227)
XLA Ops:
  0.7 2.8 %up.1 = (bf16[128,128]{1,0:T(8,128)(2,1)S(1)}, bf16[256,128]{1,0:T(8,128)(2,1)S(1)}, bf16[128,128]{1,0:T(8,128)(2,1)S(1)}, s32[128]{0:T(128)S(1)}) custom-call(s32[8]{0:T(128)} %classes_h.1, bf16[8,512,128]{2,1,0:T(8,128)(2,1)} %source.3, bf16[3,2,128,512]{3,2,1,0:T(8,128)(2,1)} %skeleton.1, bf16[8,2,128,128]{3,2,1,0:T(8,128)(2,1)} %merge.1, ...), custom_call_target="tpu_custom_call" | custom-call | flops 4294967296 | bytes 67108864 | tf_op jit(solution)/shard_map/up/pallas_call | solution.py:510
  3.4 2.5 %collective-permute-start.3 = (bf16[128,128]{1,0:T(8,128)(2,1)S(1)}, bf16[128,128]{1,0:T(8,128)(2,1)S(1)}, u32[]{:S(2)}, u32[]{:S(2)}) collective-permute-start(bf16[128,128]{1,0:T(8,128)(2,1)S(1)} %get-tuple-element.17._.own), channel_id=1, source_target_pairs={{0,3},{1,2},{2,1},{3,0},{4,7},{5,6},{6,5},{7,4},{8,11},{9,10},{10,... | collective-permute-start | bytes 98312 | tf_op jit(solution)/shard_map/ppermute | solution.py:531
  5.9 0.6 %collective-permute-start.2 = (bf16[128,128]{1,0:T(8,128)(2,1)S(1)}, bf16[128,128]{1,0:T(8,128)(2,1)S(1)}, u32[]{:S(2)}, u32[]{:S(2)}) collective-permute-start(bf16[128,128]{1,0:T(8,128)(2,1)S(1)} %get-tuple-element.17._.own), channel_id=1, source_target_pairs={{0,2},{1,3},{2,0},{3,1},{4,6},{5,7},{6,4},{7,5},{8,10},{9,11},{10,... | collective-permute-start | bytes 98312 | tf_op jit(solution)/shard_map/ppermute | solution.py:531
  6.6 4.4 %collective-permute-start.1 = (bf16[128,128]{1,0:T(8,128)(2,1)S(1)}, bf16[128,128]{1,0:T(8,128)(2,1)S(1)}, u32[]{:S(2)}, u32[]{:S(2)}) collective-permute-start(bf16[128,128]{1,0:T(8,128)(2,1)S(1)} %get-tuple-element.16), channel_id=1, source_target_pairs={{0,15},{1,2},{2,1},{3,4},{4,3},{5,6},{6,5},{7,8},{8,7},{9,10},{10,... | collective-permute-start | bytes 98312 | tf_op jit(solution)/shard_map/ppermute | solution.py:538
  11.0 0.0 copy-start
  11.0 0.0 copy-start.8
  11.1 0.0 copy-start.9
  11.1 0.0 copy-start.10
  11.1 0.0 copy-start.11
  11.1 0.0 copy-start.12
  11.1 2.3 %local.1 = (f32[8,512,128]{2,1,0:T(8,128)S(1)}, bf16[1,256,512]{2,1,0:T(8,128)(2,1)S(1)}) custom-call(s32[128]{0:T(128)S(1)} %get-tuple-element.14.table_v, bf16[8,512,128]{2,1,0:T(8,128)(2,1)S(1)} %copy-done.14, bf16[3,2,512,512]{3,2,1,0:T(8,128)(2,1)S(1)} %copy-done.13, bf16[4,2,256,256]{3,2,1,0:T(8,128)(2,1)S(1)} %copy-done.1, ...), custom_call_target="tpu_custom_call" | custom-call | flops 2147483648 | bytes 6291456 | tf_op jit(solution)/shard_map/local/pallas_call | solution.py:550
  13.4 0.0 copy-start.2
  13.4 0.0 copy-start.6
  13.4 0.0 copy-start.7
  13.5 0.0 collective-permute-done.refs_0_.joint
  13.5 0.8 %combine.1 = (bf16[128,128]{1,0:T(8,128)(2,1)S(1)}, f32[128,128]{1,0:T(8,128)S(1)}) custom-call(bf16[1,256,512]{2,1,0:T(8,128)(2,1)S(1)} %get-tuple-element.18.maps, bf16[4,2,128,256]{3,2,1,0:T(8,128)(2,1)S(1)} %copy-done, bf16[4,2,256,256]{3,2,1,0:T(8,128)(2,1)S(1)} %copy-done.1, bf16[128,128]{1,0:T(8,128)(2,1)S(1)} %get-tuple-element.17._.own, ...), custom_call_target="tpu_custom_call" | custom-call | flops 33554432 | bytes 1048576 | tf_op jit(solution)/shard_map/combine/pallas_call | solution.py:568
  14.2 0.0 copy-start.3
  14.2 0.0 copy-start.5
  14.3 0.7 %collective-permute-start.6 = (bf16[128,128]{1,0:T(8,128)(2,1)S(1)}, bf16[128,128]{1,0:T(8,128)(2,1)S(1)}, u32[]{:S(2)}, u32[]{:S(2)}) collective-permute-start(bf16[128,128]{1,0:T(8,128)(2,1)S(1)} %get-tuple-element.19._.own), channel_id=1, source_target_pairs={{0,12},{1,13},{2,14},{3,15},{4,8},{5,9},{6,10},{7,11},{8,4},{9,5},... | collective-permute-start | bytes 98312 | tf_op jit(solution)/shard_map/ppermute | solution.py:531
  15.0 3.7 %collective-permute-start.4 = (bf16[128,128]{1,0:T(8,128)(2,1)S(1)}, bf16[128,128]{1,0:T(8,128)(2,1)S(1)}, u32[]{:S(2)}, u32[]{:S(2)}) collective-permute-start(bf16[128,128]{1,0:T(8,128)(2,1)S(1)} %get-tuple-element.19._.own), channel_id=1, source_target_pairs={{0,4},{1,5},{2,6},{3,7},{4,0},{5,1},{6,2},{7,3},{8,12},{9,13},{10,... | collective-permute-start | bytes 98312 | tf_op jit(solution)/shard_map/ppermute | solution.py:531
  18.7 0.0 collective-permute-done.1.odd
  18.8 2.8 %perturb.1 = (f32[8,512,128]{2,1,0:T(8,128)S(1)}, bf16[256,1024]{1,0:T(8,128)(2,1)S(1)}) custom-call(s32[128]{0:T(128)S(1)} %get-tuple-element.14.table_v, bf16[8,512,128]{2,1,0:T(8,128)(2,1)S(1)} %copy-done.2, bf16[256,128]{1,0:T(8,128)(2,1)S(1)} %collective-permute-done.refs_0_.joint, bf16[128,128]{1,0:T(8,128)(2,1)S(1)} %collective-permute-done.1.odd, ...), custom_call_target="tpu_custom_call" | custom-call | flops 134217728 | bytes 4194304 | tf_op jit(solution)/shard_map/perturb/pallas_call | solution.py:583
  21.6 0.0 collective-permute-done.5.refs_1_
  21.6 3.4 %down.1 = (bf16[8,512,128]{2,1,0:T(8,128)(2,1)}, f32[1,8]{1,0:T(1,128)}) custom-call(s32[128]{0:T(128)S(1)} %get-tuple-element.14.table_v, bf16[256,1024]{1,0:T(8,128)(2,1)S(1)} %get-tuple-element.20.final_map, bf16[4,2,128,256]{3,2,1,0:T(8,128)(2,1)S(1)} %copy-done, bf16[128,128]{1,0:T(8,128)(2,1)S(1)} %get-tuple-element.19._.own, ...), custom_call_target="tpu_custom_call" | custom-call | flops 536870912 | bytes 8388608 | tf_op jit(solution)/shard_map/down/pallas_call | solution.py:614
  (25 shorter events, 0.1 us)
Async XLA Ops:
  0.6 10.4 %copy-start.14 = (bf16[8,512,128]{2,1,0:T(8,128)(2,1)S(1)}, bf16[8,512,128]{2,1,0:T(8,128)(2,1)}, u32[]{:S(2)}) copy-start(bf16[8,512,128]{2,1,0:T(8,128)(2,1)} %source.3) | copy-start | bytes 3145732
  0.6 10.4 %copy-start.1 = (bf16[4,2,256,256]{3,2,1,0:T(8,128)(2,1)S(1)}, bf16[4,2,256,256]{3,2,1,0:T(8,128)(2,1)}, u32[]{:S(2)}) copy-start(bf16[4,2,256,256]{3,2,1,0:T(8,128)(2,1)} %down_ref.5) | copy-start | bytes 3145732
  0.7 10.4 %copy-start.4 = (bf16[4,2,256,128]{3,2,1,0:T(8,128)(2,1)S(1)}, bf16[4,2,256,128]{3,2,1,0:T(8,128)(2,1)}, u32[]{:S(2)}) copy-start(bf16[4,2,256,128]{3,2,1,0:T(8,128)(2,1)} %parent_ref.3) | copy-start | bytes 1572868
  0.7 10.4 %copy-start.13 = (bf16[3,2,512,512]{3,2,1,0:T(8,128)(2,1)S(1)}, bf16[3,2,512,512]{3,2,1,0:T(8,128)(2,1)}, u32[]{:S(2)}) copy-start(bf16[3,2,512,512]{3,2,1,0:T(8,128)(2,1)} %solve.1) | copy-start | bytes 9437188
  3.4 10.0 %collective-permute-start.3 = (bf16[128,128]{1,0:T(8,128)(2,1)S(1)}, bf16[128,128]{1,0:T(8,128)(2,1)S(1)}, u32[]{:S(2)}, u32[]{:S(2)}) collective-permute-start(bf16[128,128]{1,0:T(8,128)(2,1)S(1)} %get-tuple-element.17._.own), channel_id=1, source_target_pairs={{0,3},{1,2},{2,1},{3,0},{4,7},{5,6},{6,5},{7,4},{8,11},{9,10},{10,... | collective-permute-start | bytes 98312 | tf_op jit(solution)/shard_map/ppermute | solution.py:531
  5.9 7.5 %collective-permute-start.2 = (bf16[128,128]{1,0:T(8,128)(2,1)S(1)}, bf16[128,128]{1,0:T(8,128)(2,1)S(1)}, u32[]{:S(2)}, u32[]{:S(2)}) collective-permute-start(bf16[128,128]{1,0:T(8,128)(2,1)S(1)} %get-tuple-element.17._.own), channel_id=1, source_target_pairs={{0,2},{1,3},{2,0},{3,1},{4,6},{5,7},{6,4},{7,5},{8,10},{9,11},{10,... | collective-permute-start | bytes 98312 | tf_op jit(solution)/shard_map/ppermute | solution.py:531
  6.6 12.1 %collective-permute-start.1 = (bf16[128,128]{1,0:T(8,128)(2,1)S(1)}, bf16[128,128]{1,0:T(8,128)(2,1)S(1)}, u32[]{:S(2)}, u32[]{:S(2)}) collective-permute-start(bf16[128,128]{1,0:T(8,128)(2,1)S(1)} %get-tuple-element.16), channel_id=1, source_target_pairs={{0,15},{1,2},{2,1},{3,4},{4,3},{5,6},{6,5},{7,8},{8,7},{9,10},{10,... | collective-permute-start | bytes 98312 | tf_op jit(solution)/shard_map/ppermute | solution.py:538
  11.0 2.5 %collective-permute-start = (bf16[256,128]{1,0:T(8,128)(2,1)S(1)}, bf16[256,128]{1,0:T(8,128)(2,1)S(1)}, u32[]{:S(2)}, u32[]{:S(2)}) collective-permute-start(bf16[256,128]{1,0:T(8,128)(2,1)S(1)} %get-tuple-element.15), channel_id=1, source_target_pairs={{0,1},{1,0},{2,3},{3,2},{4,5},{5,4},{6,7},{7,6},{8,9},{9,8},{10,11... | collective-permute-start | bytes 196616 | tf_op jit(solution)/shard_map/ppermute | solution.py:531
  11.0 2.4 %copy-start = (bf16[4,2,128,256]{3,2,1,0:T(8,128)(2,1)S(1)}, bf16[4,2,128,256]{3,2,1,0:T(8,128)(2,1)}, u32[]{:S(2)}) copy-start(bf16[4,2,128,256]{3,2,1,0:T(8,128)(2,1)} %up_ref.5) | copy-start | bytes 1572868
  11.0 7.7 %copy-start.8 = (bf16[2,128,128]{2,1,0:T(8,128)(2,1)S(1)}, bf16[2,128,128]{2,1,0:T(8,128)(2,1)}, u32[]{:S(2)}) copy-start(bf16[2,128,128]{2,1,0:T(8,128)(2,1)} %root_ref.1) | copy-start | bytes 196612
  11.1 7.7 %copy-start.9 = (f32[3,2,512]{2,1,0:T(2,128)S(1)}, f32[3,2,512]{2,1,0:T(2,128)}, u32[]{:S(2)}) copy-start(f32[3,2,512]{2,1,0:T(2,128)} %shape_ref.1) | copy-start | bytes 36868
  11.1 7.6 %copy-start.10 = (f32[128]{0:T(128)S(1)}, f32[128]{0:T(128)}, u32[]{:S(2)}) copy-start(f32[128]{0:T(128)} %param.33) | copy-start | bytes 1540
  11.1 7.6 %copy-start.11 = (f32[128]{0:T(128)S(1)}, f32[128]{0:T(128)}, u32[]{:S(2)}) copy-start(f32[128]{0:T(128)} %param.34) | copy-start | bytes 1540
  11.1 7.6 %copy-start.12 = (s32[64]{0:T(128)S(1)}, s32[64]{0:T(128)}, u32[]{:S(2)}) copy-start(s32[64]{0:T(128)} %param.35) | copy-start | bytes 772
  13.4 5.4 %copy-start.2 = (bf16[8,512,128]{2,1,0:T(8,128)(2,1)S(1)}, bf16[8,512,128]{2,1,0:T(8,128)(2,1)}, u32[]{:S(2)}) copy-start(bf16[8,512,128]{2,1,0:T(8,128)(2,1)} %forward.3) | copy-start | bytes 3145732
  13.4 5.4 %copy-start.6 = (bf16[3,2,128,128]{3,2,1,0:T(8,128)(2,1)S(1)}, bf16[3,2,128,128]{3,2,1,0:T(8,128)(2,1)}, u32[]{:S(2)}) copy-start(bf16[3,2,128,128]{3,2,1,0:T(8,128)(2,1)} %rim_left.1) | copy-start | bytes 589828
  13.4 5.3 %copy-start.7 = (bf16[3,2,128,128]{3,2,1,0:T(8,128)(2,1)S(1)}, bf16[3,2,128,128]{3,2,1,0:T(8,128)(2,1)}, u32[]{:S(2)}) copy-start(bf16[3,2,128,128]{3,2,1,0:T(8,128)(2,1)} %rim_right.1) | copy-start | bytes 589828
  14.2 7.4 %copy-start.3 = (bf16[3,2,512,128]{3,2,1,0:T(8,128)(2,1)S(1)}, bf16[3,2,512,128]{3,2,1,0:T(8,128)(2,1)}, u32[]{:S(2)}) copy-start(bf16[3,2,512,128]{3,2,1,0:T(8,128)(2,1)} %refs_5_.1) | copy-start | bytes 2359300
  14.2 7.4 %copy-start.5 = (bf16[8,2,128,128]{3,2,1,0:T(8,128)(2,1)S(1)}, bf16[8,2,128,128]{3,2,1,0:T(8,128)(2,1)}, u32[]{:S(2)}) copy-start(bf16[8,2,128,128]{3,2,1,0:T(8,128)(2,1)} %refs_4_.1) | copy-start | bytes 1572868
  14.3 7.3 %collective-permute-start.6 = (bf16[128,128]{1,0:T(8,128)(2,1)S(1)}, bf16[128,128]{1,0:T(8,128)(2,1)S(1)}, u32[]{:S(2)}, u32[]{:S(2)}) collective-permute-start(bf16[128,128]{1,0:T(8,128)(2,1)S(1)} %get-tuple-element.19._.own), channel_id=1, source_target_pairs={{0,12},{1,13},{2,14},{3,15},{4,8},{5,9},{6,10},{7,11},{8,4},{9,5},... | collective-permute-start | bytes 98312 | tf_op jit(solution)/shard_map/ppermute | solution.py:531
  15.0 6.6 %collective-permute-start.5 = (bf16[128,128]{1,0:T(8,128)(2,1)S(1)}, bf16[128,128]{1,0:T(8,128)(2,1)S(1)}, u32[]{:S(2)}, u32[]{:S(2)}) collective-permute-start(bf16[128,128]{1,0:T(8,128)(2,1)S(1)} %get-tuple-element.19._.own), channel_id=1, source_target_pairs={{0,8},{1,9},{2,10},{3,11},{4,12},{5,13},{6,14},{7,15},{8,0},{9,1},... | collective-permute-start | bytes 98312 | tf_op jit(solution)/shard_map/ppermute | solution.py:531
  15.0 6.6 %collective-permute-start.4 = (bf16[128,128]{1,0:T(8,128)(2,1)S(1)}, bf16[128,128]{1,0:T(8,128)(2,1)S(1)}, u32[]{:S(2)}, u32[]{:S(2)}) collective-permute-start(bf16[128,128]{1,0:T(8,128)(2,1)S(1)} %get-tuple-element.19._.own), channel_id=1, source_target_pairs={{0,4},{1,5},{2,6},{3,7},{4,0},{5,1},{6,2},{7,3},{8,12},{9,13},{10,... | collective-permute-start | bytes 98312 | tf_op jit(solution)/shard_map/ppermute | solution.py:531

commit v3 on v2

v3 whole, which is shorter than its diff:
```python
import functools
import math

import jax
import jax.numpy as jnp
from jax import lax
from jax.experimental import pallas as pl
from jax.experimental.pallas import tpu as pltpu
from jax.sharding import PartitionSpec as P

F32 = jnp.float32
BF16 = jnp.bfloat16
MIB = 1 << 20
VM = pl.BlockSpec(memory_space=pltpu.VMEM)
HBM = pl.BlockSpec(memory_space=pltpu.HBM)


def params(mib):
    return pltpu.CompilerParams(vmem_limit_bytes=mib * MIB)


def cost(flops, nbytes):
    return pl.CostEstimate(flops=flops, bytes_accessed=nbytes, transcendentals=0)


def half_sign(width):
    lane = lax.broadcasted_iota(jnp.int32, (1, width), 1)
    return jnp.where(lane < width // 2, -1.0, 1.0).astype(F32)


def turn(values):
    width = values.shape[-1]
    return pltpu.roll(values, width // 2, 1) * half_sign(width)


def dot(a, b):
    return jnp.dot(a, b, preferred_element_type=F32)


def split(x):
    high = x.astype(BF16)
    return high, (x - high.astype(F32)).astype(BF16)


def embed(re, im):
    return jnp.concatenate(
        [jnp.concatenate([re, -im], axis=1), jnp.concatenate([im, re], axis=1)], axis=0
    )


def times(re, im, stacked):
    left = embed(re, im)
    if stacked.dtype == BF16:
        return dot(left, stacked)
    high, low = split(stacked)
    return dot(left, high) + dot(left, low)


def side_by_side(stacked):
    rows = stacked.shape[0] // 2
    return jnp.concatenate([stacked[:rows], stacked[rows:]], axis=1)


def wide(ref, *at):
    return jnp.concatenate([ref[(*at, 0)], ref[(*at, 1)]], axis=1)


def tall(ref, *at):
    return jnp.concatenate([ref[(*at, 0)], ref[(*at, 1)]], axis=0)


def rows_of(ref, level, bit):
    rank = ref.shape[2] // 2
    start = pl.multiple_of(bit * rank, rank)
    return ref[level, 0, pl.ds(start, rank), :], ref[level, 1, pl.ds(start, rank), :]


def turned(value):
    return turn(value.astype(F32)).astype(BF16)


def slot_count(cells, classes):
    return (cells + classes) // 2


def table_size(slots):
    return -(-(3 * slots + 3) // 128) * 128


class Pairs:
    def __init__(self, table, slots):
        self.table, self.slots = table, slots

    def ends(self):
        return self.table[3 * self.slots + 1], self.table[3 * self.slots + 2]

    def __getitem__(self, slot):
        return tuple(self.table[i * self.slots + slot] for i in range(3))

    def used(self):
        return self.table[3 * self.slots]


def fill_pairs(scal, table, cells, classes):
    slots = slot_count(cells, classes)
    slot = jnp.int32(0)
    for k in range(classes):
        half = jnp.int32(0)
        for p in range(cells):
            mine = scal[p] == k

            @pl.when(jnp.logical_and(mine, half == 0))
            def _first(k=k, p=p, slot=slot):
                table[slot] = k
                table[slots + slot] = p

            @pl.when(mine)
            def _second(p=p, slot=slot):
                table[2 * slots + slot] = p

            step = mine.astype(jnp.int32)
            slot = slot + step * half
            half = jnp.where(mine, 1 - half, half)
        slot = slot + half
    table[3 * slots] = slot
    table[3 * slots + 1] = scal[0]
    table[3 * slots + 2] = scal[cells - 1]
    for s in range((cells + 1) // 2, slots):

        @pl.when(s >= slot)
        def _spare(s=s):
            for i in range(3):
                table[i * slots + s] = table[i * slots]


def up_kernel(
    classes_h,
    source,
    skeleton,
    merge,
    forward,
    joint,
    table_out,
    src_v,
    scal,
    table,
    skel_v,
    merge_v,
    cell_v,
    sems,
):
    cells, nodes, width = src_v.shape
    classes = skel_v.shape[0]
    rank = skel_v.shape[2]
    rim = (joint.shape[0] - rank) // 2
    parity = lax.axis_index("loop") & 1
    copies = []

    def start(src, dst, i):
        c = pltpu.make_async_copy(src, dst, sems.at[i])
        c.start()
        copies.append(c)

    start(classes_h, scal, 0)
    start(skeleton, skel_v, 1)
    start(source, src_v, 2)
    start(merge, merge_v, 3)
    last = (cells - 1, nodes - rim)
    even_cell = jnp.where(parity == 0, last[0], 0)
    even_row = pl.multiple_of(jnp.where(parity == 0, last[1], 0), rim)
    odd_cell = jnp.where(parity == 1, last[0], 0)
    odd_row = pl.multiple_of(jnp.where(parity == 1, last[1], 0), rim)
    start(forward.at[even_cell, pl.ds(even_row, rim), :], joint.at[pl.ds(rank, rim), :], 4)
    start(forward.at[odd_cell, pl.ds(odd_row, rim), :], joint.at[pl.ds(rank + rim, rim), :], 5)
    copies[0].wait()
    fill_pairs(scal, table, cells, classes)
    start(table, table_out, 6)
    slots = slot_count(cells, classes)
    pairs = Pairs(table, slots)
    copies[1].wait()
    copies[2].wait()
    for s in range(slots):
        k, a, b = pairs[s]
        both = dot(tall(skel_v, k), jnp.concatenate([src_v[a], src_v[b]], axis=1))
        for i, p in enumerate((a, b)):
            part = both[:, i * width : (i + 1) * width]
            for j, piece in enumerate(split(part[:rank] + turn(part[rank:]))):
                cell_v[j, p] = piece
    copies[3].wait()
    total = None
    for p in range(0, cells, 2):
        mine = range(p, min(p + 2, cells))
        left = jnp.concatenate(
            [jnp.concatenate([merge_v[i, part] for i in mine], axis=1) for part in range(2)], axis=0
        )
        for j in range(2):
            term = dot(left, jnp.concatenate([cell_v[j, i] for i in mine], axis=0))
            total = term if total is None else total + term
    joint[:rank, :] = (total[:rank] + turn(total[rank:])).astype(BF16)
    for c in copies[4:]:
        c.wait()


def fetch_table(table_v, table, sem):
    copy = pltpu.make_async_copy(table_v, table, sem.at[0])
    copy.start()
    return copy


def maps_kernel(up_ref, down_ref, parent_ref, root_ref, _, maps):
    levels = up_ref.shape[0]
    position = lax.axis_index("loop")

    def bit(level):
        return (position >> level) & 1

    for level in range(1, levels):
        total = jnp.concatenate(rows_of(down_ref, level, bit(level)), axis=0)
        if level == levels - 1:
            above = times(root_ref[0], root_ref[1], tall(up_ref, level))
            re, im = rows_of(parent_ref, level, bit(level))
            total = total.astype(F32) + times(re, im, above)
        for lower in reversed(range(level)):
            re, im = rows_of(parent_ref, lower, bit(lower))
            total = times(re, im, total)
        maps[level - 1] = jnp.concatenate(split(side_by_side(total)), axis=0)


def local_kernel(table_v, source, solve, _, local, table, table_sem):
    fetched = fetch_table(table_v, table, table_sem)
    cells, nodes, width = source.shape
    slots = slot_count(cells, solve.shape[0])
    fetched.wait()
    pairs = Pairs(table, slots)
    for s in range(slots):
        k, a, b = pairs[s]
        va, vb = source[a], source[b]
        right = jnp.concatenate(
            [
                jnp.concatenate([va, vb], axis=1),
                jnp.concatenate([turned(va), turned(vb)], axis=1),
            ],
            axis=0,
        )
        value = dot(wide(solve, k), right)
        local[a] = value[:, :width]
        local[b] = value[:, width:]


def sibling_stack(level, own, arrived, nodes_v):
    rank, width = nodes_v.shape[1:]
    mine = (lax.axis_index("loop") >> level) & 1
    for ref, where in ((own, mine), (arrived, 1 - mine)):
        value = ref[:rank, :]
        nodes_v[where] = value
        nodes_v[2 + where] = turned(value)
    return nodes_v[...].reshape(4 * rank, width)


def combine_kernel(maps, up_ref, own, arrived, *refs, level):
    (joint, part, nodes_v), before = refs[-3:], refs[:-3]
    rank = nodes_v.shape[1]
    rim = joint.shape[0] - rank
    joint[rank:, :] = arrived[arrived.shape[0] - rim :, :]
    stack = sibling_stack(level, own, arrived, nodes_v)
    joint[:rank, :] = dot(wide(up_ref, level), stack).astype(BF16)
    if level == 0:
        bit = lax.axis_index("loop") & 1
        part[...] = dot(jnp.concatenate(rows_of(maps, 0, bit), axis=1), stack)
    else:
        both = dot(maps[level - 1], stack)
        part[...] = before[0][...] + both[:rank] + both[rank:]


def rows_kernel(
    classes_ref, rim_left, rim_right, shape_ref, angle_ref, weight_ref, ids_ref, _, columns, edge_map, rows_out, scal, sem, *, device_count
):
    fetched = fetch_table(classes_ref, scal, sem)
    classes, _, nodes, width = columns.shape
    position = lax.axis_index("loop")
    ids = jnp.concatenate([ids_ref[...], ids_ref[...]], axis=1)
    entries = angle_ref.shape[1]
    chosen = lax.broadcasted_iota(jnp.int32, (entries, width), 0) == ids

    def looked_up(row):
        column = jnp.transpose(jnp.broadcast_to(row, (8, entries)))[:, :1]
        return jnp.sum(jnp.where(chosen, column, 0.0), axis=0, keepdims=True)

    scale = half_sign(width) * (-1.0 / math.sqrt(nodes * (width // 2)))
    weights = looked_up(weight_ref[...]) * scale
    angles = looked_up(angle_ref[...])
    at_start, at_end = position == 0, position == device_count - 1
    cosine = jnp.where(jnp.logical_or(at_start, at_end), jnp.cos(angles), 1.0)
    sine = jnp.sin(angles)
    sine = jnp.where(at_start, -sine, jnp.where(at_end, sine, 0.0))
    for i, row in enumerate((weights, cosine, sine)):
        rows_out[i] = jnp.broadcast_to(row, (8, width))
    for k in range(classes):
        flipped = jnp.transpose(jnp.concatenate([shape_ref[k]] * 4, axis=0))
        columns[k, 0] = jnp.broadcast_to(flipped[:, 0:1], (nodes, width)) * weights
        columns[k, 1] = jnp.broadcast_to(flipped[:, 1:2], (nodes, width)) * weights

    cells = scal.shape[0]
    fetched.wait()
    first, last = scal[0], scal[cells - 1]

    @pl.when((position & 1) == 0)
    def _left():
        edge_map[...] = wide(rim_left, first)

    @pl.when((position & 1) == 1)
    def _right():
        edge_map[...] = wide(rim_right, last)


def perturb_kernel(table_v, forward, joint_in, rim_left, rim_right, columns, rows, _, weighted, table, table_sem):
    fetched = fetch_table(table_v, table, table_sem)
    cells, nodes, width = forward.shape
    rim = rim_left.shape[-1]
    rank = joint_in.shape[0] - 2 * rim
    classes = rim_left.shape[0]
    parity = lax.axis_index("loop") & 1
    weights = rows[0, :1]
    even = joint_in[rank : rank + rim, :]
    none = jnp.zeros_like(even)
    before = jnp.where(parity == 1, even, none)
    after = jnp.where(parity == 0, even, none)

    def left_input(p):
        return jnp.where(p == 0, before, forward[jnp.maximum(p - 1, 0), nodes - rim :, :])

    def right_input(p):
        return jnp.where(p == cells - 1, after, forward[jnp.minimum(p + 1, cells - 1), :rim, :])

    def stacked(values):
        return jnp.concatenate(
            [
                jnp.concatenate(values, axis=1),
                jnp.concatenate([turned(v) for v in values], axis=1),
            ],
            axis=0,
        )

    slots = slot_count(cells, classes)
    pairs = Pairs(table, slots)
    fetched.wait()
    for s in range(slots):
        k, a, b = pairs[s]
        left = dot(wide(rim_left, k), stacked([left_input(a), left_input(b)]))
        right = dot(wide(rim_right, k), stacked([right_input(a), right_input(b)]))
        for i, p in enumerate((a, b)):
            field = forward[p].astype(F32)
            value = columns[k, 0] * field + columns[k, 1] * turn(field)
            lanes = slice(i * width, (i + 1) * width)
            weighted[p, :rim, :] = value[:rim] + left[:, lanes] * weights
            weighted[p, rim : nodes - rim, :] = value[rim : nodes - rim]
            weighted[p, nodes - rim :, :] = value[nodes - rim :] + right[:, lanes] * weights


def odd_block(edges, position, rim):
    value = None
    for level in reversed(range(1, len(edges) + 1)):
        ref = edges[level - 1]
        rows = ref[ref.shape[0] - rim :, :]
        here = ((position >> level) & 1) != (position & 1)
        value = rows if value is None else jnp.where(here, rows, value)
    return value


def down_kernel(table_v, maps, edge_map, rows_ref, own, arrived, *refs, level):
    edges, refs = refs[: level - 1] + (arrived,), refs[level - 1 :]
    part, split_ref, lift, local, weighted, adjoint, gradient = refs[:7]
    nodes_v, cell_v, out_v, sums, sems, table, table_sem = refs[7:]
    fetched = fetch_table(table_v, table, table_sem)
    rank = nodes_v.shape[1]
    cells, nodes, width = local.shape
    position = lax.axis_index("loop")
    rim = edge_map.shape[0]
    block = odd_block(edges, position, rim)
    edge = dot(edge_map[...], jnp.concatenate([block, turned(block)], axis=0))
    edge = (edge * rows_ref[1, :1] + turn(edge) * rows_ref[2, :1]) * rows_ref[0, :1]
    stack = sibling_stack(level, own, arrived, nodes_v)
    halves = dot(maps[level - 1], stack)
    field = halves[:rank] + halves[rank:] + part[...]
    both, rest = split(jnp.concatenate([field, turn(field)], axis=0))
    for p in range(cells):
        cell = dot(wide(split_ref, p), both) + dot(wide(split_ref, p), rest)
        cell_v[p] = jnp.concatenate([cell.astype(BF16), turn(cell).astype(BF16)], axis=0)

    slots = slot_count(cells, lift.shape[0])
    pairs = Pairs(table, slots)
    fetched.wait()

    def send(p):
        return pltpu.make_async_copy(out_v.at[p], adjoint.at[p], sems.at[p])

    def lift_pair(s):
        k, a, b = pairs[s]
        value = dot(wide(lift, k), jnp.concatenate([cell_v[a], cell_v[b]], axis=1))
        for i, p in enumerate((a, b)):
            rounded = (local[p] + value[:, i * width : (i + 1) * width]).astype(BF16)
            out_v[p] = rounded
            total = jnp.sum(rounded.astype(F32) * weighted[p], axis=0, keepdims=True)
            sums[p] = jnp.broadcast_to(total, (8, width))
        send(a).start()

        @pl.when(a != b)
        def _():
            send(b).start()

    for s in range(slots):
        if s < (cells + 1) // 2:
            lift_pair(s)
        else:
            pl.when(s < pairs.used())(functools.partial(lift_pair, s))

    parity = position & 1
    edge_cell = jnp.where(parity == 0, 0, cells - 1)
    edge_row = pl.multiple_of(jnp.where(parity == 0, 0, nodes - rim), rim)
    outer = out_v[edge_cell, pl.ds(edge_row, rim), :].astype(F32)
    sums[edge_cell] += jnp.broadcast_to(jnp.sum(outer * edge, axis=0, keepdims=True), (8, width))
    rows = jnp.concatenate([sums[p, :1] for p in range(cells)], axis=0)
    row = lax.broadcasted_iota(jnp.int32, (cells, cells), 0)
    lane = lax.broadcasted_iota(jnp.int32, (cells, cells), 1)
    across = jnp.sum(rows, axis=1, keepdims=True)
    gradient[...] = jnp.sum(jnp.where(row == lane, across, 0.0), axis=0, keepdims=True)
    for p in range(cells):
        send(p).wait()


def shards(
    classes,
    forward_field,
    adjoint_source,
    leaf_solve,
    leaf_lift,
    leaf_skeleton,
    block_merge,
    block_split,
    level_up,
    level_down,
    level_parent,
    root_solve,
    rim_left,
    rim_right,
    shape_derivative,
    illum_angle,
    illum_weight,
    illum_ids,
):
    position = lax.axis_index("loop")
    device_count = lax.axis_size("loop")
    cells, nodes, width = adjoint_source.shape
    class_count = leaf_solve.shape[0]
    rank = root_solve.shape[-1]
    rim = rim_left.shape[-1]
    levels = level_up.shape[0]
    slots = slot_count(cells, class_count)
    sds = jax.ShapeDtypeStruct
    joint = sds((rank + rim, width), BF16)
    size = table_size(slots)
    table_scratch = [pltpu.SMEM((size,), jnp.int32), pltpu.SemaphoreType.DMA((1,))]
    pinned = functools.partial(pltpu.with_memory_space_constraint, memory_space=pltpu.HBM)
    node, table, source_v = pl.pallas_call(
        up_kernel,
        out_shape=(
            sds((rank + 2 * rim, width), BF16),
            sds((size,), jnp.int32),
            sds((cells, nodes, width), BF16),
        ),
        in_specs=[HBM] * 5,
        out_specs=(VM,) * 3,
        scratch_shapes=[
            pltpu.SMEM((cells,), jnp.int32),
            pltpu.SMEM((size,), jnp.int32),
            pltpu.VMEM((class_count, 2, rank, nodes), BF16),
            pltpu.VMEM(block_merge.shape, BF16),
            pltpu.VMEM((2, cells, rank, width), BF16),
            pltpu.SemaphoreType.DMA((7,)),
        ],
        compiler_params=params(8),
        cost_estimate=cost(64 * cells * rank * nodes * width, 64 * MIB),
        name="up",
    )(*map(pinned, (classes, adjoint_source, leaf_skeleton, block_merge, forward_field)))

    def exchange(value, level):
        pairs = [(i, i ^ (1 << level)) for i in range(device_count)]
        return lax.ppermute(value, "loop", pairs)

    def make_maps(after):
        return pl.pallas_call(
            maps_kernel,
            out_shape=sds((max(levels - 1, 1), 2 * rank, 4 * rank), BF16),
            in_specs=[VM] * 5,
            out_specs=VM,
            compiler_params=params(4),
            cost_estimate=cost(1 << 30, 4 * MIB),
            name="maps",
        )(level_up, level_down, level_parent, root_solve, after)

    def make_local(after):
        return pl.pallas_call(
            local_kernel,
            out_shape=sds((cells, nodes, width), F32),
            in_specs=[VM] * 4,
            out_specs=VM,
            scratch_shapes=table_scratch,
            compiler_params=params(4),
            cost_estimate=cost(8 * cells * nodes * nodes * width, 6 * MIB),
            name="local",
        )(table, source_v, leaf_solve, after)

    def make_rows(after):
        return pl.pallas_call(
            functools.partial(rows_kernel, device_count=device_count),
            out_shape=(
                sds((class_count, 2, nodes, width), F32),
                sds((rim, 2 * rim), BF16),
                sds((3, 8, width), F32),
            ),
            in_specs=[VM] * 8,
            out_specs=(VM,) * 3,
            scratch_shapes=[pltpu.SMEM((cells,), jnp.int32), pltpu.SemaphoreType.DMA((1,))],
            compiler_params=params(4),
            cost_estimate=cost(1 << 30, 4 * MIB),
            name="rows",
        )(
            classes,
            rim_left,
            rim_right,
            shape_derivative,
            illum_angle[None],
            illum_weight[None],
            illum_ids[None],
            after,
        )

    def make_weighted(after):
        return pl.pallas_call(
            perturb_kernel,
            out_shape=sds((cells, nodes, width), F32),
            in_specs=[VM] * 8,
            out_specs=VM,
            scratch_shapes=table_scratch,
            compiler_params=params(4),
            cost_estimate=cost(1 << 30, 4 * MIB),
            name="perturb",
        )(table, forward_field, even_in, rim_left, rim_right, columns, rows, after)

    arrived = even_in = exchange(node, 0)
    edges = []
    part = ()
    maps = make_maps(node)
    for level in range(levels - 1):
        node, *part = pl.pallas_call(
            functools.partial(combine_kernel, level=level),
            out_shape=(joint, sds((rank, width), F32)),
            in_specs=[VM] * (4 + len(part)),
            out_specs=(VM, VM),
            scratch_shapes=[pltpu.VMEM((4, rank, width), BF16)],
            compiler_params=params(4),
            cost_estimate=cost(16 * rank * rank * width, MIB),
            name="combine",
        )(maps if level else level_down, level_up, node, arrived, *part)
        arrived = exchange(node, level + 1)
        edges.append(arrived)
        last = level == levels - 2
        if level == 0:
            local = make_local(node)
        if level == 1 or (last and level < 1):
            columns, edge_map, rows = make_rows(node)
        if level == 2 or (last and level < 2):
            weighted = make_weighted(node)

    adjoint, gradient = pl.pallas_call(
        functools.partial(down_kernel, level=levels - 1),
        out_shape=(sds((cells, nodes, width), BF16), sds((1, cells), F32)),
        in_specs=[VM] * (6 + len(edges) - 1 + 5),
        out_specs=(HBM, VM),
        scratch_shapes=[
            pltpu.VMEM((4, rank, width), BF16),
            pltpu.VMEM((cells, 2 * rank, width), BF16),
            pltpu.VMEM((cells, nodes, width), BF16),
            pltpu.VMEM((cells, 8, width), F32),
            pltpu.SemaphoreType.DMA((cells,)),
        ]
        + table_scratch,
        compiler_params=params(6),
        cost_estimate=cost(8 * cells * nodes * rank * width, 8 * MIB),
        name="down",
    )(
        table,
        maps,
        edge_map,
        rows,
        node,
        arrived,
        *edges[:-1],
        *part,
        block_split,
        leaf_lift,
        local,
        weighted,
    )
    return adjoint, gradient[0]


def solution(mesh):
    return jax.shard_map(
        shards,
        mesh=mesh,
        in_specs=(
            P(("parts", "loop")),
            P(("parts", "loop"), None, None),
            P(("parts", "loop"), None, None),
            P("parts", None, None, None),
            P("parts", None, None, None),
            P("parts", None, None, None),
            P("parts", None, None, None),
            P("parts", None, None, None),
            P("parts", None, None, None),
            P("parts", None, None, None),
            P("parts", None, None, None),
            P("parts", None, None),
            P("parts", None, None, None),
            P("parts", None, None, None),
            P("parts", None, None),
            P("parts"),
            P("parts"),
            P(),
        ),
        out_specs=(P(("parts", "loop"), None, None), P(("parts", "loop"))),
        check_vma=False,
    )
```

time: 25.2 us -> 24.6 us (0.976)
  starting transfers between devices: 12 us -> 7.9 us
  waiting for transfers between devices: 0.02 us -> 2.5 us
  Pallas kernels: 12 us -> 13.2 us
    ppermute x1 -> x0, starting transfers between devices: 4.42 us -> none  [odd_exchange(): return lax.ppermute(value, 'loop', pairs)]
    ppermute x6 -> x4, waiting for transfers between devices: 0.02 us -> 2.5 us  [exchange(): return lax.ppermute(value, 'loop', pairs)]
    pallas_call x5 -> x9, Pallas kernels: 12 us -> 13.2 us  [the longest x1 3 us: shards(): pl.pallas_call(functools.partial(down_kernel, level=levels - 1), out_shap...]
    ppermute x6 -> x4, starting transfers between devices: 7.6 us -> 7.9 us  [exchange(): return lax.ppermute(value, 'loop', pairs)]
  transfers between devices with their start and end apart: 7 -> 4, of which waited for: 0 -> 3; matrix products, arithmetic and copies ran while one was open for 0% -> 0% of each run, Pallas kernels for 23% -> 26%
where the time goes in v3:
time: 24.6 us; the launch traced here: 24.5 us
  Pallas kernels  13.2 us (54%)
  starting transfers between devices  7.9 us (32%)
  waiting for transfers between devices  2.5 us (10%)
  between operations  0.82 us (3%)
    ppermute x4, starting transfers between devices, exchange(): return lax.ppermute(value, 'loop', pairs)  7.9 us
    pallas_call x1, Pallas kernels, shards(): pl.pallas_call(functools.partial(down_kernel, level=levels - 1), out_shap...  3 us
    pallas_call x1, Pallas kernels, shards(): pl.pallas_call(up_kernel, out_shape=(sds((rank + 2 * rim, width), BF16),...  2.9 us
    ppermute x4, waiting for transfers between devices, exchange(): return lax.ppermute(value, 'loop', pairs)  2.5 us
    pallas_call x1, Pallas kernels, make_local(): pl.pallas_call(local_kernel, out_shape=sds((cells, nodes, width), F32), i...  2.24 us
    pallas_call x1, Pallas kernels, make_weighted(): pl.pallas_call(perturb_kernel, out_shape=sds((cells, nodes, width), F32),...  1.67 us
    pallas_call x1, Pallas kernels, make_maps(): pl.pallas_call(maps_kernel, out_shape=sds((max(levels - 1, 1), 2 * rank,...  1.36 us
    pallas_call x1, Pallas kernels, make_rows(): pl.pallas_call(functools.partial(rows_kernel, device_count=device_count),...  1.01 us
  transfers between devices with their start and end apart: 4, of which 3 were waited for; matrix products, arithmetic and copies ran while one was open for 0% of the time, Pallas kernels for 26%

profile of v3, /device:TPU:0, one launch (start us, length us, event | category | flops | bytes accessed | tf_op | source)
XLA Modules:
  0.0 24.5 jit_solution(9561468534022995799)
XLA Ops:
  0.6 0.0 copy-start
  0.7 2.9 %up.1 = (bf16[384,128]{1,0:T(8,128)(2,1)S(1)}, s32[128]{0:T(128)S(1)}, bf16[8,512,128]{2,1,0:T(8,128)(2,1)S(1)}) custom-call(s32[8]{0:T(128)} %classes_ref.1, bf16[8,512,128]{2,1,0:T(8,128)(2,1)} %source.1, bf16[3,2,128,512]{3,2,1,0:T(8,128)(2,1)} %skeleton.1, bf16[8,2,128,128]{3,2,1,0:T(8,128)(2,1)} %merge.1, bf16[8,512,128]{2,1,0:T(8,128)(2,1)} %forward.3), custom_call_target="tpu_custom_call" | custom-call | flops 4294967296 | bytes 67108864 | tf_op jit(solution)/shard_map/up/pallas_call | solution.py:464
  3.6 0.0 copy-start.7
  3.6 0.6 %collective-permute-start = (bf16[384,128]{1,0:T(8,128)(2,1)S(1)}, bf16[384,128]{1,0:T(8,128)(2,1)S(1)}, u32[]{:S(2)}, u32[]{:S(2)}) collective-permute-start(bf16[384,128]{1,0:T(8,128)(2,1)S(1)} %get-tuple-element.17._.own), channel_id=1, source_target_pairs={{0,1},{1,0},{2,3},{3,2},{4,5},{5,4},{6,7},{7,6},{8,9},{9,8},{10,11... | collective-permute-start | bytes 294920 | tf_op jit(solution)/shard_map/ppermute | solution.py:488
  4.2 1.4 %maps.2 = bf16[3,256,512]{2,1,0:T(8,128)(2,1)S(1)} custom-call(bf16[4,2,128,256]{3,2,1,0:T(8,128)(2,1)S(1)} %copy-done, bf16[4,2,256,256]{3,2,1,0:T(8,128)(2,1)S(1)} %copy-done.1, bf16[4,2,256,128]{3,2,1,0:T(8,128)(2,1)S(1)} %copy-done.8, bf16[2,128,128]{2,1,0:T(8,128)(2,1)S(1)} %copy-done.9, bf16[384,128]{1,0:T(8,128)(2,1)S(1)} %get-tuple-element.17._.own), custom_call_target="tpu_custom_call" | custom-call | flops 1073741824 | bytes 4194304 | tf_op jit(solution)/shard_map/maps/pallas_call | solution.py:491
  5.5 0.0 collective-permute-done.arrived.joint_in
  5.5 0.3 %combine.3 = (bf16[256,128]{1,0:T(8,128)(2,1)S(1)}, f32[128,128]{1,0:T(8,128)S(1)}) custom-call(bf16[4,2,256,256]{3,2,1,0:T(8,128)(2,1)S(1)} %copy-done.1, bf16[4,2,128,256]{3,2,1,0:T(8,128)(2,1)S(1)} %copy-done, bf16[384,128]{1,0:T(8,128)(2,1)S(1)} %get-tuple-element.17._.own, bf16[384,128]{1,0:T(8,128)(2,1)S(1)} %collective-permute-done.arrived.joint_in), custom_call_target="tpu_custom_call" | custom-call | flops 33554432 | bytes 1048576 | tf_op jit(solution)/shard_map/combine/pallas_call | solution.py:555
  5.9 2.6 %collective-permute-start.1 = (bf16[256,128]{1,0:T(8,128)(2,1)S(1)}, bf16[256,128]{1,0:T(8,128)(2,1)S(1)}, u32[]{:S(2)}, u32[]{:S(2)}) collective-permute-start(bf16[256,128]{1,0:T(8,128)(2,1)S(1)} %get-tuple-element.18.own._), channel_id=1, source_target_pairs={{0,2},{1,3},{2,0},{3,1},{4,6},{5,7},{6,4},{7,5},{8,10},{9,11},{10,... | collective-permute-start | bytes 196616 | tf_op jit(solution)/shard_map/ppermute | solution.py:488
  8.5 0.0 copy-start.11
  8.5 0.0 copy-start.12
  8.5 0.0 copy-start.13
  8.5 0.0 copy-start.14
  8.5 2.2 %local.1.refs_5_ = f32[8,512,128]{2,1,0:T(8,128)S(1)} custom-call(s32[128]{0:T(128)S(1)} %get-tuple-element.16.table_v, bf16[8,512,128]{2,1,0:T(8,128)(2,1)S(1)} %get-tuple-element.26.source, bf16[3,2,512,512]{3,2,1,0:T(8,128)(2,1)S(1)} %copy-done.7, bf16[256,128]{1,0:T(8,128)(2,1)S(1)} %get-tuple-element.18.own._), custom_call_target="tpu_custom_call" | custom-call | flops 2147483648 | bytes 6291456 | tf_op jit(solution)/shard_map/local/pallas_call | solution.py:502
  10.8 0.4 %collective-permute-done.1.arrived.refs_0_ = bf16[256,128]{1,0:T(8,128)(2,1)S(1)} collective-permute-done((bf16[256,128]{1,0:T(8,128)(2,1)S(1)}, bf16[256,128]{1,0:T(8,128)(2,1)S(1)}, u32[]{:S(2)}, u32[]{:S(2)}) %collective-permute-start.1) | collective-permute-done | bytes 65568 | tf_op jit(solution)/shard_map/ppermute | solution.py:488
  11.2 0.3 %combine.4 = (bf16[256,128]{1,0:T(8,128)(2,1)S(1)}, f32[128,128]{1,0:T(8,128)S(1)}) custom-call(bf16[3,256,512]{2,1,0:T(8,128)(2,1)S(1)} %maps.2, bf16[4,2,128,256]{3,2,1,0:T(8,128)(2,1)S(1)} %copy-done, bf16[256,128]{1,0:T(8,128)(2,1)S(1)} %get-tuple-element.18.own._, bf16[256,128]{1,0:T(8,128)(2,1)S(1)} %collective-permute-done.1.arrived.refs_0_, ...), custom_call_target="tpu_custom_call" | custom-call | flops 33554432 | bytes 1048576 | tf_op jit(solution)/shard_map/combine/pallas_call | solution.py:555
  11.6 1.9 %collective-permute-start.2 = (bf16[256,128]{1,0:T(8,128)(2,1)S(1)}, bf16[256,128]{1,0:T(8,128)(2,1)S(1)}, u32[]{:S(2)}, u32[]{:S(2)}) collective-permute-start(bf16[256,128]{1,0:T(8,128)(2,1)S(1)} %get-tuple-element.20._.own), channel_id=1, source_target_pairs={{0,4},{1,5},{2,6},{3,7},{4,0},{5,1},{6,2},{7,3},{8,12},{9,13},{10,... | collective-permute-start | bytes 196616 | tf_op jit(solution)/shard_map/ppermute | solution.py:488
  13.5 0.0 copy-start.2
  13.5 1.0 %rows.1 = (f32[3,2,512,128]{3,2,1,0:T(8,128)S(1)}, bf16[128,256]{1,0:T(8,128)(2,1)S(1)}, f32[3,8,128]{2,1,0:T(8,128)S(1)}) custom-call(s32[8]{0:T(128)S(1)} %copy-done.11, bf16[3,2,128,128]{3,2,1,0:T(8,128)(2,1)S(1)} %copy-done.5, bf16[3,2,128,128]{3,2,1,0:T(8,128)(2,1)S(1)} %copy-done.6, f32[3,2,512]{2,1,0:T(2,128)S(1)} %copy-done.10, ...), custom_call_target="tpu_custom_call" | custom-call | flops 1073741824 | bytes 4194304 | tf_op jit(solution)/shard_map/rows/pallas_call | solution.py:514
  14.5 1.4 %collective-permute-done.2.arrived.refs_1_ = bf16[256,128]{1,0:T(8,128)(2,1)S(1)} collective-permute-done((bf16[256,128]{1,0:T(8,128)(2,1)S(1)}, bf16[256,128]{1,0:T(8,128)(2,1)S(1)}, u32[]{:S(2)}, u32[]{:S(2)}) %collective-permute-start.2) | collective-permute-done | bytes 65568 | tf_op jit(solution)/shard_map/ppermute | solution.py:488
  15.9 0.4 %combine.5 = (bf16[256,128]{1,0:T(8,128)(2,1)S(1)}, f32[128,128]{1,0:T(8,128)S(1)}) custom-call(bf16[3,256,512]{2,1,0:T(8,128)(2,1)S(1)} %maps.2, bf16[4,2,128,256]{3,2,1,0:T(8,128)(2,1)S(1)} %copy-done, bf16[256,128]{1,0:T(8,128)(2,1)S(1)} %get-tuple-element.20._.own, bf16[256,128]{1,0:T(8,128)(2,1)S(1)} %collective-permute-done.2.arrived.refs_1_, ...), custom_call_target="tpu_custom_call" | custom-call | flops 33554432 | bytes 1048576 | tf_op jit(solution)/shard_map/combine/pallas_call | solution.py:555
  16.2 2.9 %collective-permute-start.3 = (bf16[256,128]{1,0:T(8,128)(2,1)S(1)}, bf16[256,128]{1,0:T(8,128)(2,1)S(1)}, u32[]{:S(2)}, u32[]{:S(2)}) collective-permute-start(bf16[256,128]{1,0:T(8,128)(2,1)S(1)} %get-tuple-element.24._.own), channel_id=1, source_target_pairs={{0,8},{1,9},{2,10},{3,11},{4,12},{5,13},{6,14},{7,15},{8,0},{9,1},... | collective-permute-start | bytes 196616 | tf_op jit(solution)/shard_map/ppermute | solution.py:488
  19.1 1.7 %perturb.1.refs_6_ = f32[8,512,128]{2,1,0:T(8,128)S(1)} custom-call(s32[128]{0:T(128)S(1)} %get-tuple-element.16.table_v, bf16[8,512,128]{2,1,0:T(8,128)(2,1)S(1)} %copy-done.2, bf16[384,128]{1,0:T(8,128)(2,1)S(1)} %collective-permute-done.arrived.joint_in, bf16[3,2,128,128]{3,2,1,0:T(8,128)(2,1)S(1)} %copy-done.5, bf16[3,2,128,128]{3,2,1,0:T(8,128)(2,1)S(1)} %copy-done.6, ...), custom_call_target="tpu_custom_call" | custom-call | flops 1073741824 | bytes 4194304 | tf_op jit(solution)/shard_map/perturb/pallas_call | solution.py:539
  20.8 0.7 %collective-permute-done.3.arrived = bf16[256,128]{1,0:T(8,128)(2,1)S(1)} collective-permute-done((bf16[256,128]{1,0:T(8,128)(2,1)S(1)}, bf16[256,128]{1,0:T(8,128)(2,1)S(1)}, u32[]{:S(2)}, u32[]{:S(2)}) %collective-permute-start.3) | collective-permute-done | bytes 65568 | tf_op jit(solution)/shard_map/ppermute | solution.py:488
  21.5 3.0 %down.1 = (bf16[8,512,128]{2,1,0:T(8,128)(2,1)}, f32[1,8]{1,0:T(1,128)}) custom-call(s32[128]{0:T(128)S(1)} %get-tuple-element.16.table_v, bf16[3,256,512]{2,1,0:T(8,128)(2,1)S(1)} %maps.2, bf16[128,256]{1,0:T(8,128)(2,1)S(1)} %get-tuple-element.21.edge_map, f32[3,8,128]{2,1,0:T(8,128)S(1)} %get-tuple-element.22.rows.rows_ref, ...), custom_call_target="tpu_custom_call" | custom-call | flops 536870912 | bytes 8388608 | tf_op jit(solution)/shard_map/down/pallas_call | solution.py:575
  (23 shorter events, 0.0 us)
Async XLA Ops:
  0.6 3.5 %copy-start = (bf16[4,2,128,256]{3,2,1,0:T(8,128)(2,1)S(1)}, bf16[4,2,128,256]{3,2,1,0:T(8,128)(2,1)}, u32[]{:S(2)}) copy-start(bf16[4,2,128,256]{3,2,1,0:T(8,128)(2,1)} %up_ref.7) | copy-start | bytes 1572868
  0.6 3.5 %copy-start.1 = (bf16[4,2,256,256]{3,2,1,0:T(8,128)(2,1)S(1)}, bf16[4,2,256,256]{3,2,1,0:T(8,128)(2,1)}, u32[]{:S(2)}) copy-start(bf16[4,2,256,256]{3,2,1,0:T(8,128)(2,1)} %maps.3) | copy-start | bytes 3145732
  0.7 3.5 %copy-start.8 = (bf16[4,2,256,128]{3,2,1,0:T(8,128)(2,1)S(1)}, bf16[4,2,256,128]{3,2,1,0:T(8,128)(2,1)}, u32[]{:S(2)}) copy-start(bf16[4,2,256,128]{3,2,1,0:T(8,128)(2,1)} %parent_ref.1) | copy-start | bytes 1572868
  0.7 3.5 %copy-start.9 = (bf16[2,128,128]{2,1,0:T(8,128)(2,1)S(1)}, bf16[2,128,128]{2,1,0:T(8,128)(2,1)}, u32[]{:S(2)}) copy-start(bf16[2,128,128]{2,1,0:T(8,128)(2,1)} %root_ref.1) | copy-start | bytes 196612
  3.6 4.9 %copy-start.7 = (bf16[3,2,512,512]{3,2,1,0:T(8,128)(2,1)S(1)}, bf16[3,2,512,512]{3,2,1,0:T(8,128)(2,1)}, u32[]{:S(2)}) copy-start(bf16[3,2,512,512]{3,2,1,0:T(8,128)(2,1)} %solve.1) | copy-start | bytes 9437188
  3.6 1.9 %collective-permute-start = (bf16[384,128]{1,0:T(8,128)(2,1)S(1)}, bf16[384,128]{1,0:T(8,128)(2,1)S(1)}, u32[]{:S(2)}, u32[]{:S(2)}) collective-permute-start(bf16[384,128]{1,0:T(8,128)(2,1)S(1)} %get-tuple-element.17._.own), channel_id=1, source_target_pairs={{0,1},{1,0},{2,3},{3,2},{4,5},{5,4},{6,7},{7,6},{8,9},{9,8},{10,11... | collective-permute-start | bytes 294920 | tf_op jit(solution)/shard_map/ppermute | solution.py:488
  5.9 5.3 %collective-permute-start.1 = (bf16[256,128]{1,0:T(8,128)(2,1)S(1)}, bf16[256,128]{1,0:T(8,128)(2,1)S(1)}, u32[]{:S(2)}, u32[]{:S(2)}) collective-permute-start(bf16[256,128]{1,0:T(8,128)(2,1)S(1)} %get-tuple-element.18.own._), channel_id=1, source_target_pairs={{0,2},{1,3},{2,0},{3,1},{4,6},{5,7},{6,4},{7,5},{8,10},{9,11},{10,... | collective-permute-start | bytes 196616 | tf_op jit(solution)/shard_map/ppermute | solution.py:488
  8.5 4.9 %copy-start.5 = (bf16[3,2,128,128]{3,2,1,0:T(8,128)(2,1)S(1)}, bf16[3,2,128,128]{3,2,1,0:T(8,128)(2,1)}, u32[]{:S(2)}) copy-start(bf16[3,2,128,128]{3,2,1,0:T(8,128)(2,1)} %rim_left.3) | copy-start | bytes 589828
  8.5 4.9 %copy-start.6 = (bf16[3,2,128,128]{3,2,1,0:T(8,128)(2,1)S(1)}, bf16[3,2,128,128]{3,2,1,0:T(8,128)(2,1)}, u32[]{:S(2)}) copy-start(bf16[3,2,128,128]{3,2,1,0:T(8,128)(2,1)} %rim_right.3) | copy-start | bytes 589828
  8.5 4.9 %copy-start.10 = (f32[3,2,512]{2,1,0:T(2,128)S(1)}, f32[3,2,512]{2,1,0:T(2,128)}, u32[]{:S(2)}) copy-start(f32[3,2,512]{2,1,0:T(2,128)} %shape_ref.1) | copy-start | bytes 36868
  8.5 4.9 %copy-start.11 = (s32[8]{0:T(128)S(1)}, s32[8]{0:T(128)}, u32[]{:S(2)}) copy-start(s32[8]{0:T(128)} %classes_ref.1) | copy-start | bytes 100
  8.5 4.9 %copy-start.12 = (f32[128]{0:T(128)S(1)}, f32[128]{0:T(128)}, u32[]{:S(2)}) copy-start(f32[128]{0:T(128)} %param.33) | copy-start | bytes 1540
  8.5 4.9 %copy-start.13 = (f32[128]{0:T(128)S(1)}, f32[128]{0:T(128)}, u32[]{:S(2)}) copy-start(f32[128]{0:T(128)} %param.34) | copy-start | bytes 1540
  8.5 4.9 %copy-start.14 = (s32[64]{0:T(128)S(1)}, s32[64]{0:T(128)}, u32[]{:S(2)}) copy-start(s32[64]{0:T(128)} %param.35) | copy-start | bytes 772
  11.6 4.3 %collective-permute-start.2 = (bf16[256,128]{1,0:T(8,128)(2,1)S(1)}, bf16[256,128]{1,0:T(8,128)(2,1)S(1)}, u32[]{:S(2)}, u32[]{:S(2)}) collective-permute-start(bf16[256,128]{1,0:T(8,128)(2,1)S(1)} %get-tuple-element.20._.own), channel_id=1, source_target_pairs={{0,4},{1,5},{2,6},{3,7},{4,0},{5,1},{6,2},{7,3},{8,12},{9,13},{10,... | collective-permute-start | bytes 196616 | tf_op jit(solution)/shard_map/ppermute | solution.py:488
  13.5 5.7 %copy-start.2 = (bf16[8,512,128]{2,1,0:T(8,128)(2,1)S(1)}, bf16[8,512,128]{2,1,0:T(8,128)(2,1)}, u32[]{:S(2)}) copy-start(bf16[8,512,128]{2,1,0:T(8,128)(2,1)} %forward.3) | copy-start | bytes 3145732
  16.2 5.2 %collective-permute-start.3 = (bf16[256,128]{1,0:T(8,128)(2,1)S(1)}, bf16[256,128]{1,0:T(8,128)(2,1)S(1)}, u32[]{:S(2)}, u32[]{:S(2)}) collective-permute-start(bf16[256,128]{1,0:T(8,128)(2,1)S(1)} %get-tuple-element.24._.own), channel_id=1, source_target_pairs={{0,8},{1,9},{2,10},{3,11},{4,12},{5,13},{6,14},{7,15},{8,0},{9,1},... | collective-permute-start | bytes 196616 | tf_op jit(solution)/shard_map/ppermute | solution.py:488
  19.1 2.4 %copy-start.3 = (bf16[3,2,512,128]{3,2,1,0:T(8,128)(2,1)S(1)}, bf16[3,2,512,128]{3,2,1,0:T(8,128)(2,1)}, u32[]{:S(2)}) copy-start(bf16[3,2,512,128]{3,2,1,0:T(8,128)(2,1)} %refs_4_.1) | copy-start | bytes 2359300
  19.1 2.4 %copy-start.4 = (bf16[8,2,128,128]{3,2,1,0:T(8,128)(2,1)S(1)}, bf16[8,2,128,128]{3,2,1,0:T(8,128)(2,1)}, u32[]{:S(2)}) copy-start(bf16[8,2,128,128]{3,2,1,0:T(8,128)(2,1)} %refs_3_.1) | copy-start | bytes 1572868
